TPU v7x, 256 devices: a whole 4x4x8 slice. The times are simulated.
256 devices in a mesh: leaf: 16 (over x, y), rows: 16 (over z, core).
Axes of the slice: x: 4, y: 4, z: 8, core: 2. Of those that a mesh axis runs over, the one named last changes fastest.
Arguments:
- rhs_top: float32 [1, 4096, 128], P(None, 'rows'), may hold values from -6 to 6
- rhs_one: float32 [2, 2048, 128], P(None, 'rows'), may hold values from -6 to 6
- rhs_two: float32 [4, 2048, 128], P(None, 'rows'), may hold values from -6 to 6
- rhs_three: float32 [8, 1024, 128], P(None, 'rows'), may hold values from -6 to 6
- inv_top: float32 [4096, 4096], P('rows', 'leaf')
- inv_one: float32 [2048, 4096], P('rows', 'leaf')
- inv_two: float32 [2048, 8192], P('rows', 'leaf')
- inv_three: float32 [1024, 8192], P('rows', 'leaf')
- panel_one: float32 [4096, 2048], P('leaf', 'rows'), may hold values from -0.0625 to 0.0625
- panel_two: float32 [8192, 4096], P('leaf', 'rows'), may hold values from -0.0625 to 0.0625
- panel_three: float32 [8192, 4096], P('leaf', 'rows'), may hold values from -0.09375 to 0.09375
- rows_one: int32 [2, 16], P(None, 'rows'), may hold values from 0 to 31, as said below
- rows_two: int32 [4, 32], P(None, 'rows'), may hold values from 0 to 47, as said below
- rows_three: int32 [8, 32], P(None, 'rows'), may hold values from 0 to 63, as said below
Outputs:
- solution_top: float32 [1, 4096, 128], P(None, 'rows')
- solution_one: float32 [2, 2048, 128], P(None, 'rows')
- solution_two: float32 [4, 2048, 128], P(None, 'rows')
- solution_three: float32 [8, 1024, 128], P(None, 'rows')
Inputs may be any that keep to these rules, and one draw needn't show every extreme that they name: `rows_one`: each row lists 16 different blocks of a chain of 32 blocks, the chain's first and last among them. `rows_two`: each row lists 32 different blocks of a chain of 48 blocks, the chain's first and last among them. `rows_three`: each row lists 32 different blocks of a chain of 64 blocks, the chain's first and last among them.
All inputs are finite; a program needn't handle non-finite values.
Results may differ from a plain program's by a relative error of at most 0.0001.
Values sent between devices are 32-bit elements; how exact they have to be, the bound alone decides.
A program may use at most 64 MiB of HBM per device.

v0:
```python
import jax
import jax.numpy as jnp
from jax import lax
from jax.sharding import PartitionSpec as P

SEP0 = 4096
SEP1 = 2048
SEP2 = 2048
SEP3 = 1024
BLOCK = 128


def layout(sep_count, sep_size):
    span_rows = sep_count * sep_size // lax.axis_size("leaf")
    held_count = max(1, span_rows // sep_size)
    part_rows = min(span_rows, sep_size)
    first_sep = lax.axis_index("leaf") * span_rows // sep_size
    return (held_count, part_rows, first_sep)


def forward_solve(inverse, source, sep_count, sep_size):
    held_count, part_rows, first_sep = layout(sep_count, sep_size)
    picked = lax.dynamic_slice_in_dim(source, first_sep, held_count, 0)
    blocks = inverse.reshape(inverse.shape[0], held_count, part_rows)
    partial_y = jnp.einsum("csr,scn->srn", blocks, picked, precision=lax.Precision.HIGHEST)
    return lax.psum(partial_y, "rows")


def chain_matches(index_rows, first_sep, held_count, chain_count, listed):
    picked_rows = lax.dynamic_slice_in_dim(index_rows, first_sep, held_count, 0)
    column_ids = lax.broadcasted_iota(jnp.int32, (held_count, chain_count, listed), 1)
    return (column_ids == picked_rows[:, None, :]).astype(jnp.float32)


def ancestor_terms(panel, index_rows, solved_rows, sep_sizes, sep_counts, level_at):
    held_count, part_rows, first_sep = layout(sep_counts[level_at], sep_sizes[level_at])
    width_rhs = solved_rows.shape[2]
    listed = panel.shape[1] // BLOCK
    chain_count = sum(sep_sizes[:level_at]) // BLOCK
    panel_cut = panel.reshape(held_count, part_rows, listed * BLOCK)
    updates = jnp.einsum("sra,srn->san", panel_cut, solved_rows, precision=lax.Precision.HIGHEST)
    matches = chain_matches(index_rows, first_sep, held_count, chain_count, listed)
    spread = jnp.einsum(
        "sck,skbn->scbn",
        matches,
        updates.reshape(held_count, listed, BLOCK, width_rhs),
        precision=lax.Precision.HIGHEST,
    )
    owners = first_sep + jnp.arange(held_count, dtype=jnp.int32)
    results = []
    offset = 0
    for upper in range(level_at):
        blocks_up = sep_sizes[upper] // BLOCK
        segment = spread[:, offset : offset + blocks_up].reshape(
            held_count, sep_sizes[upper], width_rhs
        )
        target_ids = lax.broadcasted_iota(jnp.int32, (held_count, sep_counts[upper]), 1)
        target = (target_ids == (owners >> level_at - upper)[:, None]).astype(jnp.float32)
        results.append(jnp.einsum("sq,srn->qrn", target, segment, precision=lax.Precision.HIGHEST))
        offset = offset + blocks_up
    return results


def reduce_dense(parts):
    column_parts = lax.psum_scatter(parts, "rows", scatter_dimension=1, tiled=True)
    return lax.psum(column_parts, "leaf")


def backward_panel(panel, index_rows, gathered, solved_rows, sep_sizes, sep_counts, level_at):
    held_count, part_rows, first_sep = layout(sep_counts[level_at], sep_sizes[level_at])
    width_rhs = solved_rows.shape[2]
    listed = panel.shape[1] // BLOCK
    chain_count = sum(sep_sizes[:level_at]) // BLOCK
    owners = first_sep + jnp.arange(held_count, dtype=jnp.int32)
    pieces = []
    for upper in range(level_at):
        target_ids = lax.broadcasted_iota(jnp.int32, (held_count, sep_counts[upper]), 1)
        target = (target_ids == (owners >> level_at - upper)[:, None]).astype(jnp.float32)
        pieces.append(
            jnp.einsum("sq,qrn->srn", target, gathered[upper], precision=lax.Precision.HIGHEST)
        )
    chain_x = jnp.concatenate(pieces, axis=1).reshape(held_count, chain_count, BLOCK, width_rhs)
    matches = chain_matches(index_rows, first_sep, held_count, chain_count, listed)
    chosen = jnp.einsum("sck,scbn->skbn", matches, chain_x, precision=lax.Precision.HIGHEST)
    panel_cut = panel.reshape(held_count, part_rows, listed * BLOCK)
    partial_g = jnp.einsum(
        "sra,san->srn",
        panel_cut,
        chosen.reshape(held_count, listed * BLOCK, width_rhs),
        precision=lax.Precision.HIGHEST,
    )
    return solved_rows - lax.psum(partial_g, "rows")


def backward_solve(inverse, residue, sep_count, sep_size):
    held_count, part_rows, first_sep = layout(sep_count, sep_size)
    blocks = inverse.reshape(inverse.shape[0], held_count, part_rows)
    partial_x = jnp.einsum("csr,srn->scn", blocks, residue, precision=lax.Precision.HIGHEST)
    owners = first_sep + jnp.arange(held_count, dtype=jnp.int32)
    place_ids = lax.broadcasted_iota(jnp.int32, (held_count, sep_count), 1)
    placing = (place_ids == owners[:, None]).astype(jnp.float32)
    dense = jnp.einsum("sq,scn->qcn", placing, partial_x, precision=lax.Precision.HIGHEST)
    return lax.psum(dense, "leaf")


def body(
    rhs_top,
    rhs_one,
    rhs_two,
    rhs_three,
    inv_top,
    inv_one,
    inv_two,
    inv_three,
    panel_one,
    panel_two,
    panel_three,
    rows_one,
    rows_two,
    rows_three,
):
    sep_sizes = [SEP0, SEP1, SEP2, SEP3]
    sep_counts = [1, 2, 4, 8]
    right_sides = [rhs_top, rhs_one, rhs_two, rhs_three]
    inverses = [inv_top, inv_one, inv_two, inv_three]
    panels = [None, panel_one, panel_two, panel_three]
    indices = [None, rows_one, rows_two, rows_three]
    solved = [None, None, None, None]
    owed_rows = [jnp.zeros(item.shape, jnp.float32) for item in right_sides]
    for level_at in (3, 2, 1, 0):
        source = right_sides[level_at] - owed_rows[level_at]
        solved[level_at] = forward_solve(
            inverses[level_at], source, sep_counts[level_at], sep_sizes[level_at]
        )
        if level_at > 0:
            fresh = ancestor_terms(
                panels[level_at],
                indices[level_at],
                solved[level_at],
                sep_sizes,
                sep_counts,
                level_at,
            )
            reduced = reduce_dense(tuple(fresh))
            for upper in range(level_at):
                owed_rows[upper] = owed_rows[upper] + reduced[upper]
    gathered = []
    results = []
    for level_at in range(4):
        residue = solved[level_at]
        if level_at > 0:
            residue = backward_panel(
                panels[level_at],
                indices[level_at],
                gathered,
                solved[level_at],
                sep_sizes,
                sep_counts,
                level_at,
            )
        solution_cols = backward_solve(
            inverses[level_at], residue, sep_counts[level_at], sep_sizes[level_at]
        )
        results.append(solution_cols)
        if level_at < 3:
            gathered.append(lax.all_gather(solution_cols, "rows", axis=1, tiled=True))
    return (results[0], results[1], results[2], results[3])


def solution(mesh):
    return jax.shard_map(
        body,
        mesh=mesh,
        in_specs=(
            P(None, "rows", None),
            P(None, "rows", None),
            P(None, "rows", None),
            P(None, "rows", None),
            P("rows", "leaf"),
            P("rows", "leaf"),
            P("rows", "leaf"),
            P("rows", "leaf"),
            P("leaf", "rows"),
            P("leaf", "rows"),
            P("leaf", "rows"),
            P(None, "rows"),
            P(None, "rows"),
            P(None, "rows"),
        ),
        out_specs=(
            P(None, "rows", None),
            P(None, "rows", None),
            P(None, "rows", None),
            P(None, "rows", None),
        ),
        check_vma=False,
    )
```

profile of v0, /device:TPU:25, one launch (start us, length us, event | category | flops | bytes accessed | tf_op | source)
XLA Modules:
  0.0 1857.3 jit_solution(8080732922114036708)
XLA Ops:
  7.2 2.1 convolution_bitcast_fusion.5
  10.3 113.1 %all-reduce.15.cloned.1.call-done = f32[1,512,128]{1,2,0:T(8,128)} async-done(((f32[1,512,128]{1,2,0:T(8,128)}), f32[1,512,128]{1,2,0:T(8,128)}) %all-reduce.15.cloned.1.call-update) | async-done | bytes 262160 | tf_op jit(solution)/shard_map/psum | solution.py:26
  125.2 1.9 convolution_bitcast_fusion
  127.3 1.8 copy-done.1
  129.4 2.3 broadcast_multiply_fusion
  131.8 60.6 %reduce-scatter.4.cloned.1.call-done = f32[4,128,128]{2,1,0:T(8,128)} async-done(((f32[4,2048,128]{2,1,0:T(8,128)}), f32[4,128,128]{2,1,0:T(8,128)}) %reduce-scatter.4.cloned.1.call-update) | async-done | bytes 262160 | tf_op jit(solution)/shard_map/reduce_scatter | solution.py:65
  192.6 97.5 %all-reduce.17.cloned.1.call-done = f32[4,128,128]{2,1,0:T(8,128)} async-done(((f32[4,128,128]{2,1,0:T(8,128)}), f32[4,128,128]{2,1,0:T(8,128)}) %all-reduce.17.cloned.1.call-update) | async-done | bytes 262160 | tf_op jit(solution)/shard_map/psum | solution.py:66
  290.1 2.0 convolution_bitcast_fusion.4
  292.7 111.9 %all-reduce.19.cloned.1.call-done = f32[1,512,128]{1,2,0:T(8,128)} async-done(((f32[1,512,128]{1,2,0:T(8,128)}), f32[1,512,128]{1,2,0:T(8,128)}) %all-reduce.19.cloned.1.call-update) | async-done | bytes 262160 | tf_op jit(solution)/shard_map/psum | solution.py:26
  406.2 1.5 convolution_bitcast_fusion.1
  409.4 1.7 multiply_add_fusion
  411.2 57.7 %reduce-scatter.6.cloned.1.call-done = f32[2,128,128]{2,1,0:T(8,128)} async-done(((f32[2,2048,128]{2,1,0:T(8,128)}), f32[2,128,128]{2,1,0:T(8,128)}) %reduce-scatter.6.cloned.1.call-update) | async-done | bytes 131088 | tf_op jit(solution)/shard_map/reduce_scatter | solution.py:65
  470.2 94.2 %all-reduce.39.cloned.1.call-done = f32[2,128,128]{2,1,0:T(8,128)} async-done(((f32[2,128,128]{2,1,0:T(8,128)}), f32[2,128,128]{2,1,0:T(8,128)}) %all-reduce.39.cloned.1.call-update) | async-done | bytes 131088 | tf_op jit(solution)/shard_map/psum | solution.py:66
  564.5 1.8 convolution_bitcast_fusion.10
  566.3 2.8 fusion.2
  570.3 108.3 %all-reduce.21.cloned.1.call-done = f32[1,256,128]{1,2,0:T(8,128)} async-done(((f32[1,256,128]{1,2,0:T(8,128)}), f32[1,256,128]{1,2,0:T(8,128)}) %all-reduce.21.cloned.1.call-update) | async-done | bytes 131088 | tf_op jit(solution)/shard_map/psum | solution.py:26
  680.1 1.6 bitcast_add_fusion
  681.8 57.6 %reduce-scatter.8.cloned.1.call-done = f32[1,256,128]{2,1,0:T(8,128)} async-done(((f32[1,4096,128]{2,1,0:T(8,128)}), f32[1,256,128]{2,1,0:T(8,128)}) %reduce-scatter.8.cloned.1.call-update) | async-done | bytes 131088 | tf_op jit(solution)/shard_map/reduce_scatter | solution.py:65
  739.5 95.6 %all-reduce.41.cloned.1.call-done = f32[1,256,128]{2,1,0:T(8,128)} async-done(((f32[1,256,128]{2,1,0:T(8,128)}), f32[1,256,128]{2,1,0:T(8,128)}) %all-reduce.41.cloned.1.call-update) | async-done | bytes 131088 | tf_op jit(solution)/shard_map/psum | solution.py:66
  835.1 2.0 convolution_bitcast_fusion.6
  837.1 112.0 %all-reduce.23.cloned.1.call-done = f32[256,128]{0,1:T(8,128)} async-done(((f32[256,128]{0,1:T(8,128)}), f32[256,128]{0,1:T(8,128)}) %all-reduce.23.cloned.1.call-update) | async-done | bytes 131088 | tf_op jit(solution)/shard_map/psum | solution.py:26
  949.1 2.0 fusion.7
  951.1 93.2 %all-reduce.25.cloned.1.call-done = f32[1,256,128]{1,2,0:T(8,128)} async-done(((f32[1,256,128]{1,2,0:T(8,128)}), f32[1,256,128]{1,2,0:T(8,128)}) %all-reduce.25.cloned.1.call-update) | async-done | bytes 131088 | tf_op jit(solution)/shard_map/psum | solution.py:103
  1044.6 43.0 %all-gather.4.cloned.1.call-done = f32[1,4096,128]{1,2,0:T(8,128)} async-done(((f32[1,256,128]{1,2,0:T(8,128)}), f32[1,4096,128]{1,2,0:T(8,128)}) %all-gather.4.cloned.1.call-update) | async-done | bytes 2097168 | tf_op jit(solution)/shard_map/all_gather | solution.py:166
  1087.6 3.7 broadcast_multiply_fusion.1
  1094.2 107.6 %all-reduce.27.cloned.1.call-done = f32[1,256,128]{1,2,0:T(8,128)} async-done(((f32[1,256,128]{1,2,0:T(8,128)}), f32[1,256,128]{1,2,0:T(8,128)}) %all-reduce.27.cloned.1.call-update) | async-done | bytes 131088 | tf_op jit(solution)/shard_map/psum | solution.py:92
  1203.9 92.9 %all-reduce.29.cloned.1.call-done = f32[2,128,128]{2,1,0:T(8,128)} async-done(((f32[2,128,128]{2,1,0:T(8,128)}), f32[2,128,128]{2,1,0:T(8,128)}) %all-reduce.29.cloned.1.call-update) | async-done | bytes 131088 | tf_op jit(solution)/shard_map/psum | solution.py:103
  1296.9 43.2 %all-gather.6.cloned.1.call-done = f32[2,2048,128]{2,1,0:T(8,128)} async-done(((f32[2,128,128]{2,1,0:T(8,128)}), f32[2,2048,128]{2,1,0:T(8,128)}) %all-gather.6.cloned.1.call-update) | async-done | bytes 2097168 | tf_op jit(solution)/shard_map/all_gather | solution.py:166
  1340.1 7.6 fusion.5
  1347.7 3.6 copy.42
  1352.8 2.2 copy.47
  1355.0 3.6 copy.34
  1358.5 3.0 fusion.33
  1363.1 107.9 %all-reduce.31.cloned.1.call-done = f32[1,512,128]{1,2,0:T(8,128)} async-done(((f32[1,512,128]{1,2,0:T(8,128)}), f32[1,512,128]{1,2,0:T(8,128)}) %all-reduce.31.cloned.1.call-update) | async-done | bytes 262160 | tf_op jit(solution)/shard_map/psum | solution.py:92
  1473.2 94.5 %all-reduce.33.cloned.1.call-done = f32[4,128,128]{2,1,0:T(8,128)} async-done(((f32[4,128,128]{2,1,0:T(8,128)}), f32[4,128,128]{2,1,0:T(8,128)}) %all-reduce.33.cloned.1.call-update) | async-done | bytes 262160 | tf_op jit(solution)/shard_map/psum | solution.py:103
  1567.7 11.6 all-reduce.35.cloned.1.call-start
  1579.3 6.6 fusion.3
  1585.9 1.9 copy.43
  1587.8 25.7 %all-gather.8.cloned.1.call-done = f32[4,2048,128]{2,1,0:T(8,128)} async-done(((f32[4,128,128]{2,1,0:T(8,128)}), f32[4,2048,128]{2,1,0:T(8,128)}) %all-gather.8.cloned.1.call-update) | async-done | bytes 4194320 | tf_op jit(solution)/shard_map/all_gather | solution.py:166
  1613.5 9.6 fusion
  1623.1 3.8 copy.45
  1626.9 1.9 maximum_bitcast_fusion
  1628.8 2.7 copy.48
  1631.5 5.5 copy.37
  1637.0 3.7 fusion.36
  1642.3 108.3 %all-reduce.35.cloned.1.call-done = f32[1,512,128]{1,2,0:T(8,128)} async-done(((f32[1,512,128]{1,2,0:T(8,128)}), f32[1,512,128]{1,2,0:T(8,128)}) %all-reduce.35.cloned.1.call-update) | async-done | bytes 262160 | tf_op jit(solution)/shard_map/psum | solution.py:92
  1753.4 93.8 %all-reduce.37.cloned.1.call-done = f32[8,64,128]{2,1,0:T(8,128)} async-done(((f32[8,64,128]{2,1,0:T(8,128)}), f32[8,64,128]{2,1,0:T(8,128)}) %all-reduce.37.cloned.1.call-update) | async-done | bytes 262160 | tf_op jit(solution)/shard_map/psum | solution.py:103
  1848.6 1.7 copy.71
  (122 shorter events, 27.8 us)
Async XLA Ops:
  7.2 397.4 %copy-start = (f32[512,256]{1,0:T(8,128)S(1)}, f32[512,256]{1,0:T(8,128)}, u32[]{:S(2)}) copy-start(f32[512,256]{1,0:T(8,128)} %param.23) | copy-start | bytes 1572868
  7.2 116.2 %all-reduce.15.cloned.1.call-start = ((), (), s32[]{:S(2)}) async-start(), calls=%async_computation.3 | async-start | bytes 524288 | tf_op jit(solution)/shard_map/psum | solution.py:26
  9.4 183.1 %reduce-scatter.4.cloned.1.call-start = ((), (), s32[]{:S(2)}) async-start(), calls=%async_computation.4 | async-start | bytes 4456448 | tf_op jit(solution)/shard_map/reduce_scatter | solution.py:65
  127.1 1.9 copy-start.1
  131.7 158.3 %copy-start.8 = (f32[128,512]{1,0:T(8,128)S(1)}, f32[128,512]{1,0:T(8,128)}, u32[]{:S(2)}) copy-start(f32[128,512]{1,0:T(8,128)} %param.20) | copy-start | bytes 786436
  131.7 160.4 %copy-start.18 = (s32[4,2]{0,1:T(2,128)S(1)}, s32[4,2]{0,1:T(2,128)}, u32[]{:S(2)}) copy-start(s32[4,2]{0,1:T(2,128)} %param.26) | copy-start | bytes 100
  131.8 158.3 %all-reduce.17.cloned.1.call-start = ((), (), s32[]{:S(2)}) async-start(), calls=%async_computation.5 | async-start | bytes 524288 | tf_op jit(solution)/shard_map/psum | solution.py:66
  192.5 212.1 %all-reduce.19.cloned.1.call-start = ((), (), s32[]{:S(2)}) async-start(), calls=%async_computation.6 | async-start | bytes 524288 | tf_op jit(solution)/shard_map/psum | solution.py:26
  292.1 176.8 %reduce-scatter.6.cloned.1.call-start = ((), (), s32[]{:S(2)}) async-start(), calls=%async_computation.21 | async-start | bytes 2228224 | tf_op jit(solution)/shard_map/reduce_scatter | solution.py:65
  407.7 1.7 copy-start.2
  411.1 57.9 %copy-start.19 = (s32[2,1]{0,1:T(1,128)S(1)}, s32[2,1]{0,1:T(1,128)}, u32[]{:S(2)}) copy-start(s32[2,1]{0,1:T(1,128)} %param.25) | copy-start | bytes 28
  411.1 153.4 %copy-start.10 = (f32[128,256]{1,0:T(8,128)S(1)}, f32[128,256]{1,0:T(8,128)}, u32[]{:S(2)}) copy-start(f32[128,256]{1,0:T(8,128)} %param.19) | copy-start | bytes 393220
  411.1 153.4 %copy-start.17 = (f32[2,128,128]{2,1,0:T(8,128)S(1)}, f32[2,128,128]{2,1,0:T(8,128)}, u32[]{:S(2)}) copy-start(f32[2,128,128]{2,1,0:T(8,128)} %param.15) | copy-start | bytes 393220
  411.1 153.3 %all-reduce.39.cloned.1.call-start = ((), (), s32[]{:S(2)}) async-start(), calls=%async_computation.19 | async-start | bytes 262144 | tf_op jit(solution)/shard_map/psum | solution.py:66
  468.9 209.7 %all-reduce.21.cloned.1.call-start = ((), (), s32[]{:S(2)}) async-start(), calls=%async_computation.7 | async-start | bytes 262144 | tf_op jit(solution)/shard_map/psum | solution.py:26
  566.3 173.1 %reduce-scatter.8.cloned.1.call-start = ((), (), s32[]{:S(2)}) async-start(), calls=%async_computation.22 | async-start | bytes 2228224 | tf_op jit(solution)/shard_map/reduce_scatter | solution.py:65
  569.1 109.5 %copy-start.12 = (f32[256,128]{1,0:T(8,128)S(1)}, f32[256,128]{1,0:T(8,128)}, u32[]{:S(2)}) copy-start(f32[256,128]{1,0:T(8,128)} %param.22) | copy-start | bytes 393220
  681.8 153.3 %copy-start.7 = (f32[256,256]{1,0:T(8,128)S(1)}, f32[256,256]{1,0:T(8,128)}, u32[]{:S(2)}) copy-start(f32[256,256]{1,0:T(8,128)} %param.18) | copy-start | bytes 786436
  681.8 153.3 %copy-start.16 = (f32[1,256,128]{2,1,0:T(8,128)S(1)}, f32[1,256,128]{2,1,0:T(8,128)}, u32[]{:S(2)}) copy-start(f32[1,256,128]{2,1,0:T(8,128)} %param.14) | copy-start | bytes 393220
  681.8 153.3 %all-reduce.41.cloned.1.call-start = ((), (), s32[]{:S(2)}) async-start(), calls=%async_computation.20 | async-start | bytes 262144 | tf_op jit(solution)/shard_map/psum | solution.py:66
  739.4 209.7 %all-reduce.23.cloned.1.call-start = ((), (), s32[]{:S(2)}) async-start(), calls=%async_computation.8 | async-start | bytes 262144 | tf_op jit(solution)/shard_map/psum | solution.py:26
  837.0 207.2 %all-reduce.25.cloned.1.call-start = ((), (), s32[]{:S(2)}) async-start(), calls=%async_computation.9 | async-start | bytes 262144 | tf_op jit(solution)/shard_map/psum | solution.py:103
  951.1 136.5 %all-gather.4.cloned.1.call-start = ((), (), s32[]{:S(2)}) async-start(), calls=%async_computation.10 | async-start | bytes 2228224 | tf_op jit(solution)/shard_map/all_gather | solution.py:166
  1044.3 157.5 %all-reduce.27.cloned.1.call-start = ((), (), s32[]{:S(2)}) async-start(), calls=%async_computation.11 | async-start | bytes 262144 | tf_op jit(solution)/shard_map/psum | solution.py:92
  1091.7 110.1 %copy-start.11 = (f32[1,256,128]{1,2,0:T(8,128)S(1)}, f32[1,256,128]{1,2,0:T(8,128)}, u32[]{:S(2)}) copy-start(f32[1,256,128]{1,2,0:T(8,128)} %all-reduce.21.cloned.1.call-done) | copy-start | bytes 393220
  1094.1 202.7 %all-reduce.29.cloned.1.call-start = ((), (), s32[]{:S(2)}) async-start(), calls=%async_computation.12 | async-start | bytes 262144 | tf_op jit(solution)/shard_map/psum | solution.py:103
  1203.8 136.3 %all-gather.6.cloned.1.call-start = ((), (), s32[]{:S(2)}) async-start(), calls=%async_computation.13 | async-start | bytes 2228224 | tf_op jit(solution)/shard_map/all_gather | solution.py:166
  1296.8 174.1 %all-reduce.31.cloned.1.call-start = ((), (), s32[]{:S(2)}) async-start(), calls=%async_computation.14 | async-start | bytes 524288 | tf_op jit(solution)/shard_map/psum | solution.py:92
  1358.5 112.4 %copy-start.6 = (f32[1,512,128]{1,2,0:T(8,128)S(1)}, f32[1,512,128]{1,2,0:T(8,128)}, u32[]{:S(2)}) copy-start(f32[1,512,128]{1,2,0:T(8,128)} %all-reduce.19.cloned.1.call-done) | copy-start | bytes 786436
  1363.0 204.7 %all-reduce.33.cloned.1.call-start = ((), (), s32[]{:S(2)}) async-start(), calls=%async_computation.15 | async-start | bytes 524288 | tf_op jit(solution)/shard_map/psum | solution.py:103
  1473.2 140.3 %all-gather.8.cloned.1.call-start = ((), (), s32[]{:S(2)}) async-start(), calls=%async_computation.16 | async-start | bytes 4456448 | tf_op jit(solution)/shard_map/all_gather | solution.py:166
  1567.7 182.8 %all-reduce.35.cloned.1.call-start = ((), (), s32[]{:S(2)}) async-start(), calls=%async_computation.17 | async-start | bytes 524288 | tf_op jit(solution)/shard_map/psum | solution.py:92
  1623.1 3.8 copy-start.3
  1636.9 3.8 copy-start.4
  1637.0 113.6 %copy-start.5 = (f32[1,512,128]{1,2,0:T(8,128)S(1)}, f32[1,512,128]{1,2,0:T(8,128)}, u32[]{:S(2)}) copy-start(f32[1,512,128]{1,2,0:T(8,128)} %all-reduce.15.cloned.1.call-done) | copy-start | bytes 786436
  1637.0 113.6 %copy-start.15 = (f32[64,512]{1,0:T(8,128)S(1)}, f32[64,512]{1,0:T(8,128)}, u32[]{:S(2)}) copy-start(f32[64,512]{1,0:T(8,128)} %param.21) | copy-start | bytes 393220
  1640.7 112.0 %copy-start.13 = (f32[1,256,128]{1,2,0:T(8,128)S(1)}, f32[1,256,128]{1,2,0:T(8,128)}, u32[]{:S(2)}) copy-start(f32[1,256,128]{1,2,0:T(8,128)} %all-reduce.25.cloned.1.call-done) | copy-start | bytes 393220
  1640.7 206.6 %copy-start.14 = (f32[2,128,128]{2,1,0:T(8,128)S(1)}, f32[2,128,128]{2,1,0:T(8,128)}, u32[]{:S(2)}) copy-start(f32[2,128,128]{2,1,0:T(8,128)} %all-reduce.29.cloned.1.call-done) | copy-start | bytes 393220
  1640.7 207.2 %copy-start.9 = (f32[4,128,128]{2,1,0:T(8,128)S(1)}, f32[4,128,128]{2,1,0:T(8,128)}, u32[]{:S(2)}) copy-start(f32[4,128,128]{2,1,0:T(8,128)} %all-reduce.33.cloned.1.call-done) | copy-start | bytes 786436
  1642.2 205.1 %all-reduce.37.cloned.1.call-start = ((), (), s32[]{:S(2)}) async-start(), calls=%async_computation.18 | async-start | bytes 524288 | tf_op jit(solution)/shard_map/psum | solution.py:103
Sparse Core Ops, SparseCore 0:
  10.9 112.5 all-reduce.14
  131.9 60.5 reduce-scatter.3
  195.6 94.3 all-reduce.16
  292.8 111.7 all-reduce.18
  411.2 57.5 reduce-scatter.5
  471.9 92.4 all-reduce.38
  567.3 111.2 all-reduce.20
  681.9 57.4 reduce-scatter.7
  742.6 92.4 all-reduce.40
  837.8 111.2 all-reduce.22
  952.9 91.3 all-reduce.24
  1046.0 41.5 all-gather.3
  1094.2 107.5 all-reduce.26
  1205.4 91.3 all-reduce.28
  1298.5 41.5 all-gather.5
  1363.1 107.7 all-reduce.30
  1474.5 93.1 all-reduce.32
  1569.4 44.0 all-gather.7
  1642.3 108.1 all-reduce.34
  1754.1 93.1 all-reduce.36
where the time goes:
time: 1870 us; the launch traced here: 1860 us
  waiting for transfers between devices  1720 us (92%)
  matrix products  56.9 us (3%)
  local copies, waits for them, and re-layouts  35.2 us (2%)
  other arithmetic  18.7 us (1%)
    psum x4, waiting for transfers between devices, forward_solve(): return lax.psum(partial_y, 'rows')  445 us
    psum x4, waiting for transfers between devices, backward_solve(): return lax.psum(dense, 'leaf')  374 us
    psum x3, waiting for transfers between devices, backward_panel(): return solved_rows - lax.psum(partial_g, 'rows')  324 us
    psum x3, waiting for transfers between devices, reduce_dense(): return lax.psum(column_parts, 'leaf')  287 us
    reduce_scatter x3, waiting for transfers between devices, reduce_dense(): lax.psum_scatter(parts, 'rows', scatter_dimension=1, tiled=True)  176 us
    all_gather x3, waiting for transfers between devices, body(): gathered.append(lax.all_gather(solution_cols, 'rows', axis=1, tiled=True))  112 us
  transfers between devices with their start and end apart: 20, of which 20 were waited for; matrix products, arithmetic and copies ran while one was open for 1% of the time, Pallas kernels for 0%

commit v1 on v0

v1 whole, which is shorter than its diff:
```python
import jax
import jax.numpy as jnp
from jax import lax
from jax.experimental import pallas as pl
from jax.experimental.pallas import tpu as pltpu
from jax.sharding import PartitionSpec as P

F32 = jnp.float32
BF16 = jnp.bfloat16
NR = 16
NL = 16
N = 128
MESH = pl.DeviceIdType.MESH

BUFS = {}
PHASES = []


def _pair(name, m):
    BUFS["c_" + name] = (8, m, N)
    BUFS["d_" + name] = (8, m, N)
    PHASES.append(name + "_c")


def _rows_ar(name, m):
    if m == 32:
        BUFS["a_" + name] = (8, 2, m, N)
        BUFS["b_" + name] = (8, m, N)
        BUFS["y_" + name] = (8, 2, m, N)
        _pair(name + "_rs", m)
        PHASES.append(name + "_ag_c")
    else:
        BUFS["a_" + name] = (NR, m, N)
        BUFS["b_" + name] = (NR, m, N)
        BUFS["y_" + name] = (NR, m, N)
    PHASES.extend([name + "_rs", name + "_ag"])


for _name, _m in (("f3", 32), ("f2", 32), ("f1", 16), ("f0", 16), ("g1", 16), ("g2", 32), ("g3", 32)):
    _rows_ar(_name, _m)
for _name, _g, _h in (("two", 4, 32), ("one", 8, 16), ("top", 16, 16)):
    if _h == 32:
        _pair(_name + "_rs", _h)
    BUFS["n_" + _name] = (8, 2, _h, N) if _h == 32 else (NR, _h, N)
    BUFS["m_" + _name] = (8, _h, N) if _h == 32 else (NR, _h, N)
    BUFS["w_" + _name] = (_g, _h, N)
    PHASES.extend([_name + "_rs", _name + "_ag"])
BUFS.update(
    u3=(2, 8, 16, N),
    u2=(2, 8, 16, N),
    u1=(8, 16, N),
    ru32=(4, 2, 2, 16, N),
    ru31=(8, 2, 16, N),
    ru21=(8, 2, 16, N),
    ru30=(16, 2, 16, N),
    ru20=(16, 2, 16, N),
    ru10=(16, 16, N),
    bins0=(NR, 16, N),
    bins1=(NR, 16, N),
    x0p=(16, 16, N),
    x0l=(16, 16, N),
    x0r=(NR, 16, N),
    x0o=(16, 16, N),
    s10=(2, 16, N),
    s20=(4, 2, 16, N),
    s30=(8, 2, 16, N),
    t10=(16, 16, N),
    t20=(16, 2, 16, N),
    t30=(16, 2, 16, N),
    x1p=(8, 16, N),
    x1l=(8, 16, N),
    x1r=(NR, 16, N),
    x1o=(16, 16, N),
    s21=(2, 2, 16, N),
    s31=(4, 2, 16, N),
    t21=(8, 2, 16, N),
    t31=(8, 2, 16, N),
    x2p=(4, 32, N),
    x2l=(4, 32, N),
    x2r=(8, 2, 32, N),
    x2o=(16, 32, N),
    s32=(2, 2, 32, N),
    t32=(4, 2, 32, N),
    x3p=(2, 32, N),
    x3l=(2, 32, N),
    x3o=(16, 32, N),
)
PHASES.extend(("u32", "u31", "u21", "u30", "u20", "u10", "x0l", "x0r", "x0o", "t10", "t20", "t30"))
PHASES.extend(("x1l", "x1r", "x1o", "t21", "t31", "x2l", "x2r", "x2o", "t32", "x3l", "x3o", "x2r_c"))
BUF_NAMES = list(BUFS)
PHASE_ID = {name: at for at, name in enumerate(PHASES)}
WEIGHTS = (
    ("i0", (256, 256)),
    ("i1", (128, 256)),
    ("i2", (128, 512)),
    ("i3", (64, 512)),
    ("p1", (256, 128)),
    ("p2", (512, 256)),
    ("p3", (512, 256)),
)
RIGHT = ((256, N), (128, N), (128, N), (64, N))


def split(value):
    high = value.astype(BF16)
    return high, (value - high.astype(F32)).astype(BF16)


def kernel(*refs):
    rhs_in = refs[:4]
    weight_in = dict(zip([name for name, _ in WEIGHTS], refs[4:11]))
    r1, r2, r3 = refs[11:14]
    out0, out1, out2, out3 = refs[14:18]
    buf = dict(zip(BUF_NAMES, refs[18 : 18 + len(BUF_NAMES)]))
    at = 18 + len(BUF_NAMES)
    whi = dict(zip([name for name, _ in WEIGHTS], refs[at : at + 7]))
    wlo = dict(zip([name for name, _ in WEIGHTS], refs[at + 7 : at + 14]))
    w32 = dict(zip([name for name, _ in WEIGHTS], refs[at + 14 : at + 21]))
    rhs = refs[at + 21 : at + 25]
    load_sem, send_sem, recv_sem = refs[at + 25 :]

    leaf = lax.axis_index("leaf")
    row = lax.axis_index("rows")
    q1, q2, q3 = lax.div(leaf, 8), lax.div(leaf, 4), lax.div(leaf, 2)
    pos = {16: leaf, 8: lax.rem(leaf, 8), 4: lax.rem(leaf, 4), 2: lax.rem(leaf, 2)}

    loads = {}

    def load(name, src, dst):
        loads[name] = pltpu.make_async_copy(src, dst, load_sem.at[len(loads)])
        loads[name].start()

    load("i3", weight_in["i3"], w32["i3"])
    for at, sep in ((3, q3), (2, q2), (1, q1), (0, 0)):
        load(at, rhs_in[at].at[sep], rhs[at])
    for name in ("p3", "i2", "p2", "i1", "p1", "i0"):
        load(name, weight_in[name], w32[name])

    def ready(*names):
        for name in names:
            loads[name].wait()
            whi[name][...], wlo[name][...] = split(w32[name][...])

    z, core = lax.div(row, 2), lax.rem(row, 2)
    partner = {"rows": row + 1 - 2 * core}

    def z_peer(step):
        half = lax.div(step + 1, 2)
        sign = 1 - 2 * lax.rem(step, 2)
        return lax.rem(z + 4 + half * sign, 8)

    def row_peer(step):
        half = lax.div(step + 1, 2)
        sign = 1 - 2 * lax.rem(step, 2)
        return lax.rem(row + 8 + half * sign, NR)

    barrier = pltpu.get_barrier_semaphore()

    def hello(step, carry):
        pl.semaphore_signal(barrier, inc=1, device_id={"rows": lax.rem(row + 1 + step, NR)}, device_id_type=MESH)
        pl.semaphore_signal(barrier, inc=1, device_id={"leaf": lax.rem(leaf + 1 + step, NL)}, device_id_type=MESH)
        return carry

    lax.fori_loop(0, 15, hello, 0)

    pending = []

    def remote(src, dst, phase, device):
        return pltpu.make_async_remote_copy(
            src_ref=src,
            dst_ref=dst,
            send_sem=send_sem.at[PHASE_ID[phase]],
            recv_sem=recv_sem.at[PHASE_ID[phase]],
            device_id=device,
            device_id_type=MESH,
        )

    def rows_send(phase, src, dst, whole):
        def go(step, carry):
            peer = row_peer(step)
            remote(src(peer), dst, phase, {"rows": peer}).start()
            return carry

        lax.fori_loop(0, NR - 1, go, 0)
        pending.append((phase, whole))

    def leaf_send(phase, group, src, dst, whole):
        base = leaf - pos[group]

        def go(step, carry):
            to = lax.rem(pos[group] + 1 + step, group)
            remote(src(to), dst, phase, {"leaf": base + to}).start()
            return carry

        lax.fori_loop(0, group - 1, go, 0)
        pending.append((phase, whole))

    def arrived(phase, whole):
        remote(whole, whole, phase, {"rows": lax.rem(row + 1, NR)}).wait_recv()

    def mm(name, x, transposed):
        xh, xl = split(x)
        both = jnp.concatenate([xh, xl], axis=1)
        dims = (((0,), (0,)), ((), ())) if transposed else (((1,), (0,)), ((), ()))
        first = lax.dot_general(whi[name][...], both, dims, preferred_element_type=F32)
        second = lax.dot_general(wlo[name][...], xh, dims, preferred_element_type=F32)
        return first[:, :N] + first[:, N:] + second

    def total(ref, count):
        terms = [ref[j] for j in range(count)]
        while len(terms) > 1:
            terms = [a + b for a, b in zip(terms[::2], terms[1::2])]
        return terms[0]

    def z_send(phase, src, dst, whole):
        def go(step, carry):
            peer = z_peer(step)
            remote(src(peer), dst, phase, {"rows": 2 * peer + core}).start()
            return carry

        lax.fori_loop(0, 7, go, 0)
        pending.append((phase, whole))

    def pair_reduce(phase, out, land, fill=None):
        other, both = buf["c_" + phase], buf["d_" + phase]
        remote(out.at[:, 1 - core], other, phase + "_c", partner).start()
        pending.append((phase + "_c", other))
        arrived(phase + "_c", other)
        both[...] = out[:, core] + other[...]
        some = land.at[pl.ds(0, 7)]
        z_send(phase, lambda peer: both.at[peer], land.at[z], some)
        land[z] = both[z]
        if fill is not None:
            fill()
        arrived(phase, some)
        return total(land, 8)

    def pair_gather(phase, piece, full, fill=None):
        full[z, core] = piece
        some = full.at[pl.ds(0, 7), 0]
        z_send(phase, lambda peer: full.at[z, core], full.at[z, core], some)
        if fill is not None:
            fill()
        arrived(phase, some)
        mine = full.at[:, core]
        remote(mine, mine, phase + "_c", partner).start()
        pending.append((phase + "_c", mine))
        arrived(phase + "_c", mine)

    def rows_reduce(phase, out, land, fill=None):
        some = land.at[pl.ds(0, NR - 1)]
        rows_send(phase, lambda peer: out.at[peer], land.at[row], some)
        land[row] = out[row]
        if fill is not None:
            fill()
        arrived(phase, some)
        return total(land, NR)

    def rows_gather(phase, piece, full, fill=None):
        full[row] = piece
        some = full.at[pl.ds(0, NR - 1)]
        rows_send(phase, lambda peer: full.at[row], full.at[row], some)
        if fill is not None:
            fill()
        arrived(phase, some)

    def leaf_gather_start(phase, group, piece, full):
        full[pos[group]] = piece
        some = full.at[pl.ds(0, group - 1)]
        leaf_send(phase, group, lambda to: full.at[pos[group]], full.at[pos[group]], some)
        return some

    def leaf_gather(phase, group, piece, full):
        arrived(phase, leaf_gather_start(phase, group, piece, full))

    def leaf_exchange(phase, group, src, land, own):
        some = land.at[pl.ds(0, group - 1)]
        leaf_send(phase, group, src, land.at[pos[group]], some)
        land[pos[group]] = own
        return some

    def rows_sum(name, value, fill=None, fill2=None):
        out, land, full = buf["a_" + name], buf["b_" + name], buf["y_" + name]
        out[...] = value.reshape(out.shape)
        paired = len(out.shape) == 4
        piece = (pair_reduce if paired else rows_reduce)(name + "_rs", out, land, fill)
        (pair_gather if paired else rows_gather)(name + "_ag", piece, full, fill2)

    def rows_value(name):
        full = buf["y_" + name]
        return full[...].reshape(-1, N)

    ready("i3")
    loads[3].wait()
    first = mm("i3", rhs[3][...], True)
    pl.semaphore_wait(barrier, 30)

    def ready_two():
        ready("i2", "p2")
        loads[2].wait()
        loads[1].wait()
        loads[0].wait()

    rows_sum("f3", first, lambda: ready("p3"), ready_two)
    u3 = buf["u3"]
    u3[...] = mm("p3", rows_value("f3"), True).reshape(u3.shape)
    ru32 = buf["ru32"]
    some = leaf_exchange(
        "u32", 4, lambda to: u3.at[:, pl.ds(2 * to, 2)], ru32, u3[:, pl.ds(2 * pos[4], 2)]
    )
    arrived("u32", some)

    def bins(dst, terms, base, shape, add=None):
        for s in range(NR):
            value = None if add is None else add[s]
            for index, piece in terms:
                one = jnp.where(index == base(s), piece, jnp.zeros(shape, F32))
                value = one if value is None else value + one
            if len(dst.shape) == 4:
                dst[s // 2, s % 2] = value
            else:
                dst[s] = value

    terms = []
    for p in range(2):
        for k in range(2):
            piece = (ru32[2 * p, k] + ru32[2 * p + 1, k]).reshape(32, N)
            terms.append((r3[k, 2 * q2 + p], piece))
    bins(buf["n_two"], terms, lambda s: 48 + s, (32, N))

    ru31, ru30 = buf["ru31"], buf["ru30"]

    def start_u3_upper():
        start_u3_upper.one = leaf_exchange("u31", 8, lambda to: u3.at[:, to], ru31, u3[:, pos[8]])
        start_u3_upper.top = leaf_exchange(
            "u30", 16, lambda to: u3.at[:, lax.rem(to, 8)], ru30, u3[:, pos[8]]
        )
        ready("i1", "p1", "i0")

    piece = pair_reduce("two_rs", buf["n_two"], buf["m_two"], start_u3_upper)
    leaf_gather("two_ag", 4, piece, buf["w_two"])
    source = rhs[2][...] - buf["w_two"][...].reshape(128, N)

    def fill_one():
        arrived("u31", start_u3_upper.one)
        terms = []
        for p in range(4):
            for k in range(2):
                terms.append((r3[k, 4 * q1 + p], ru31[2 * p, k] + ru31[2 * p + 1, k]))
        bins(buf["bins1"], terms, lambda s: 32 + s, (16, N))

    def fill_top():
        arrived("u30", start_u3_upper.top)
        terms = []
        for p in range(8):
            for k in range(2):
                terms.append((r3[k, p], ru30[2 * p, k] + ru30[2 * p + 1, k]))
        bins(buf["bins0"], terms, lambda s: 2 * s + q1, (16, N))

    rows_sum("f2", mm("i2", source, True), fill_one, fill_top)
    u2 = buf["u2"]
    u2[...] = mm("p2", rows_value("f2"), True).reshape(u2.shape)
    ru21, ru20 = buf["ru21"], buf["ru20"]
    some = leaf_exchange("u21", 8, lambda to: u2.at[:, to], ru21, u2[:, pos[8]])
    arrived("u21", some)
    terms = []
    for p in range(2):
        for k in range(2):
            piece = (ru21[4 * p, k] + ru21[4 * p + 1, k]) + (ru21[4 * p + 2, k] + ru21[4 * p + 3, k])
            terms.append((r2[k, 2 * q1 + p], piece))
    bins(buf["n_one"], terms, lambda s: 32 + s, (16, N), buf["bins1"])

    def start_u2_upper():
        start_u2_upper.top = leaf_exchange(
            "u20", 16, lambda to: u2.at[:, lax.rem(to, 8)], ru20, u2[:, pos[8]]
        )

    piece = rows_reduce("one_rs", buf["n_one"], buf["m_one"], start_u2_upper)
    leaf_gather("one_ag", 8, piece, buf["w_one"])
    source = rhs[1][...] - buf["w_one"][...].reshape(128, N)

    def fill_top_two():
        arrived("u20", start_u2_upper.top)
        terms = []
        for p in range(4):
            for k in range(2):
                piece = (ru20[4 * p, k] + ru20[4 * p + 1, k]) + (ru20[4 * p + 2, k] + ru20[4 * p + 3, k])
                terms.append((r2[k, p], piece))
        bins(buf["bins0"], terms, lambda s: 2 * s + q1, (16, N), buf["bins0"])

    rows_sum("f1", mm("i1", source, True), fill_top_two)
    u1 = buf["u1"]
    u1[...] = mm("p1", rows_value("f1"), True).reshape(u1.shape)
    ru10 = buf["ru10"]
    some = leaf_exchange("u10", 16, lambda to: u1.at[lax.rem(to, 8)], ru10, u1[pos[8]])
    arrived("u10", some)
    terms = []
    for p in range(2):
        piece = ru10[8 * p]
        for j in range(1, 8):
            piece = piece + ru10[8 * p + j]
        terms.append((r1[0, p], piece))
    bins(buf["n_top"], terms, lambda s: 2 * s + q1, (16, N), buf["bins0"])
    piece = rows_reduce("top_rs", buf["n_top"], buf["m_top"])
    leaf_gather("top_ag", 16, piece, buf["w_top"])
    source = rhs[0][...] - buf["w_top"][...].reshape(256, N)

    rows_sum("f0", mm("i0", source, True))
    x0p, x0l, x0r = buf["x0p"], buf["x0l"], buf["x0r"]
    x0p[...] = mm("i0", rows_value("f0"), False).reshape(x0p.shape)
    some = leaf_exchange("x0l", 16, lambda to: x0p.at[to], x0l, x0p[leaf])
    arrived("x0l", some)
    piece = total(x0l, 16)
    rows_gather("x0r", piece, x0r)

    def pick_top(index):
        held = x0r[jnp.minimum(lax.div(index, 2), 15)]
        mine = jnp.logical_and(index < 32, lax.rem(index, 2) == q1)
        return jnp.where(mine, held, jnp.zeros((16, N), F32))

    s10, t10 = buf["s10"], buf["t10"]
    for p in range(2):
        s10[p] = pick_top(r1[0, p])
    some = leaf_exchange("t10", 16, lambda to: s10.at[lax.div(to, 8)], t10, s10[q1])
    wait_x0o = leaf_gather_start("x0o", 16, piece, buf["x0o"])
    arrived("t10", some)
    chosen = (t10[pl.ds(0, 8)] + t10[pl.ds(8, 8)]).reshape(128, N)

    s20, t20, s30, t30 = buf["s20"], buf["t20"], buf["s30"], buf["t30"]

    def fill_t():
        for p in range(4):
            for k in range(2):
                s20[p, k] = pick_top(r2[k, p])
        fill_t.two = leaf_exchange("t20", 16, lambda to: s20.at[lax.div(to, 4)], t20, s20[q2])
        for p in range(8):
            for k in range(2):
                s30[p, k] = pick_top(r3[k, p])
        fill_t.three = leaf_exchange("t30", 16, lambda to: s30.at[lax.div(to, 2)], t30, s30[q3])

    rows_sum("g1", mm("p1", chosen, False), fill_t)
    x1p, x1l, x1r = buf["x1p"], buf["x1l"], buf["x1r"]
    x1p[...] = mm("i1", rows_value("f1") - rows_value("g1"), False).reshape(x1p.shape)
    some = leaf_exchange("x1l", 8, lambda to: x1p.at[to], x1l, x1p[pos[8]])
    arrived("x1l", some)
    piece = total(x1l, 8)
    rows_gather("x1r", piece, x1r)

    def pick_one(index):
        held = x1r[jnp.clip(index - 32, 0, 15)]
        mine = jnp.logical_and(index >= 32, index < 48)
        return jnp.where(mine, held, jnp.zeros((16, N), F32))

    s21, t21, s31, t31 = buf["s21"], buf["t21"], buf["s31"], buf["t31"]
    for p in range(2):
        for k in range(2):
            s21[p, k] = pick_one(r2[k, 2 * q1 + p])
    some = leaf_exchange("t21", 8, lambda to: s21.at[lax.div(to, 4)], t21, s21[q2 - 2 * q1])
    wait_x1o = leaf_gather_start("x1o", 16, piece, buf["x1o"])
    arrived("t20", fill_t.two)
    arrived("t21", some)
    parts = []
    for k in range(2):
        parts.append(
            (t20[pl.ds(0, 8), k] + t20[pl.ds(8, 8), k] + t21[pl.ds(0, 8), k]).reshape(128, N)
        )

    def fill_o():
        for p in range(4):
            for k in range(2):
                s31[p, k] = pick_one(r3[k, 4 * q1 + p])
        fill_o.three = leaf_exchange(
            "t31", 8, lambda to: s31.at[lax.div(to, 2)], t31, s31[q3 - 4 * q1]
        )

    rows_sum("g2", mm("p2", jnp.concatenate(parts, axis=0), False), fill_o)
    x2p, x2l, x2r = buf["x2p"], buf["x2l"], buf["x2r"]
    x2p[...] = mm("i2", rows_value("f2") - rows_value("g2"), False).reshape(x2p.shape)
    some = leaf_exchange("x2l", 4, lambda to: x2p.at[to], x2l, x2p[pos[4]])
    arrived("x2l", some)
    piece = total(x2l, 4)
    pair_gather("x2r", piece, x2r)

    def pick_two(index):
        at = jnp.clip(index - 48, 0, 15)
        held = x2r[lax.div(at, 2), lax.rem(at, 2)]
        return jnp.where(index >= 48, held, jnp.zeros((32, N), F32))

    s32, t32 = buf["s32"], buf["t32"]
    for p in range(2):
        for k in range(2):
            s32[p, k] = pick_two(r3[k, 2 * q2 + p])
    some = leaf_exchange("t32", 4, lambda to: s32.at[lax.div(to, 2)], t32, s32[q3 - 2 * q2])
    wait_x2o = leaf_gather_start("x2o", 16, piece, buf["x2o"])
    arrived("t30", fill_t.three)
    arrived("t31", fill_o.three)
    arrived("t32", some)
    parts = []
    for k in range(2):
        upper = t30[pl.ds(0, 8), k] + t30[pl.ds(8, 8), k] + t31[pl.ds(0, 8), k]
        parts.append(upper.reshape(128, N) + t32[pl.ds(0, 4), k].reshape(128, N))

    def outputs():
        arrived("x0o", wait_x0o)
        out0[...] = buf["x0o"][...].reshape(out0.shape)
        arrived("x1o", wait_x1o)
        out1[...] = buf["x1o"][...].reshape(out1.shape)
        arrived("x2o", wait_x2o)
        out2[...] = buf["x2o"][...].reshape(out2.shape)

    rows_sum("g3", mm("p3", jnp.concatenate(parts, axis=0), False), outputs)
    x3p, x3l = buf["x3p"], buf["x3l"]
    x3p[...] = mm("i3", rows_value("f3") - rows_value("g3"), False).reshape(x3p.shape)
    some = leaf_exchange("x3l", 2, lambda to: x3p.at[to], x3l, x3p[pos[2]])
    arrived("x3l", some)
    leaf_gather("x3o", 16, total(x3l, 2), buf["x3o"])
    out3[...] = buf["x3o"][...].reshape(out3.shape)

    for phase, whole in pending:
        remote(whole, whole, phase, {"rows": lax.rem(row + 1, NR)}).wait_send()


def store(*refs):
    copies = [pltpu.make_async_copy(refs[j], refs[4 + j], refs[8].at[j]) for j in range(4)]
    for copy in copies:
        copy.start()
    for copy in copies:
        copy.wait()


def body(*args):
    vmem = pl.BlockSpec(memory_space=pltpu.VMEM)
    smem = pl.BlockSpec(memory_space=pltpu.SMEM)
    outs = tuple(jax.ShapeDtypeStruct(item.shape, F32) for item in args[:4])
    solved = tuple(
        pl.pallas_call(
            kernel,
            out_shape=outs,
            in_specs=[pl.BlockSpec(memory_space=pltpu.MemorySpace.HBM)] * 11 + [smem] * 3,
            out_specs=[vmem] * 4,
            scratch_shapes=[pltpu.VMEM(BUFS[name], F32) for name in BUF_NAMES]
            + [pltpu.VMEM(shape, BF16) for _, shape in WEIGHTS] * 2
            + [pltpu.VMEM(shape, F32) for _, shape in WEIGHTS]
            + [pltpu.VMEM(shape, F32) for shape in RIGHT]
            + [pltpu.SemaphoreType.DMA((11,))]
            + [pltpu.SemaphoreType.DMA((len(PHASES),)), pltpu.SemaphoreType.DMA((len(PHASES),))],
            compiler_params=pltpu.CompilerParams(
                collective_id=0, has_side_effects=True, vmem_limit_bytes=60 * 1024 * 1024
            ),
        )(*args[:11], *(item.T for item in args[11:]))
    )
    return tuple(
        pl.pallas_call(
            store,
            out_shape=outs,
            in_specs=[vmem] * 4,
            out_specs=[pl.BlockSpec(memory_space=pltpu.MemorySpace.HBM)] * 4,
            scratch_shapes=[pltpu.SemaphoreType.DMA((4,))],
        )(*solved)
    )


def solution(mesh):
    rhs = P(None, "rows", None)
    return jax.shard_map(
        body,
        mesh=mesh,
        in_specs=(rhs,) * 4
        + (P("rows", "leaf"),) * 4
        + (P("leaf", "rows"),) * 3
        + (P(None, "rows"),) * 3,
        out_specs=(rhs,) * 4,
        check_vma=False,
    )
```

time: 1870 us -> 200 us (0.11)
  waiting for transfers between devices: 1720 us -> 0 us
  Pallas kernels: 0 us -> 198 us
  matrix products: 56.9 us -> 0 us
  local copies, waits for them, and re-layouts: 35.2 us -> 0 us
  other arithmetic: 18.7 us -> 0 us
    psum x14 -> x0, waiting for transfers between devices: 1430 us -> none  [the longest x4 445 us: forward_solve(): return lax.psum(partial_y, 'rows')]
    pallas_call x0 -> x2, Pallas kernels: none -> 198 us  [the longest x1 196 us: body(): pl.pallas_call(kernel, out_shape=outs, in_specs=[pl.BlockSpec(memory_spac...]
    reduce_scatter x3 -> x0, waiting for transfers between devices: 176 us -> none  [reduce_dense(): lax.psum_scatter(parts, 'rows', scatter_dimension=1, tiled=True)]
    all_gather x3 -> x0, waiting for transfers between devices: 112 us -> none  [body(): gathered.append(lax.all_gather(solution_cols, 'rows', axis=1, tiled=True))]
    dot_general x22 -> x0, matrix products: 56.9 us -> none  [the longest x3 23.7 us: backward_panel(): jnp.einsum('sq,qrn->srn', target, gathered[upper], precision=lax.Precisio...]
  transfers between devices with their start and end apart: 20 -> 0, of which waited for: 20 -> 0; matrix products, arithmetic and copies ran while one was open for 1% -> 0% of each run, Pallas kernels for 0% -> 0%
where the time goes in v1:
time: 200 us; the launch traced here: 199 us
  Pallas kernels  198 us (99%)
    pallas_call x1, Pallas kernels, body(): pl.pallas_call(kernel, out_shape=outs, in_specs=[pl.BlockSpec(memory_spac...  196 us

profile of v1, /device:TPU:25, one launch (start us, length us, event | category | flops | bytes accessed | tf_op | source)
XLA Modules:
  0.0 199.1 jit_solution(563830879690044443)
XLA Ops:
  0.6 196.4 %shard_map.165 = (f32[1,256,128]{2,1,0:T(8,128)}, f32[2,128,128]{2,1,0:T(8,128)}, f32[4,128,128]{2,1,0:T(8,128)}, f32[8,64,128]{2,1,0:T(8,128)}) custom-call(f32[1,256,128]{2,1,0:T(8,128)} %refs_0_.1, f32[2,128,128]{2,1,0:T(8,128)} %refs_1_.1, f32[4,128,128]{2,1,0:T(8,128)} %refs_2_.1, f32[8,64,128]{2,1,0:T(8,128)} %refs_3_.1, f32[256,256]{1,0:T(8,128)} %refs_4_.1, ...), custom_call_target="tpu_custom_call" | custom-call | tf_op jit(solution)/shard_map/pallas_call | solution.py:536
  197.1 2.1 %shard_map.166 = (f32[1,256,128]{2,1,0:T(8,128)}, f32[2,128,128]{2,1,0:T(8,128)}, f32[4,128,128]{2,1,0:T(8,128)}, f32[8,64,128]{2,1,0:T(8,128)}) custom-call(f32[1,256,128]{2,1,0:T(8,128)} %get-tuple-element.8.refs_0_, f32[2,128,128]{2,1,0:T(8,128)} %get-tuple-element.9.refs_1_, f32[4,128,128]{2,1,0:T(8,128)} %get-tuple-element.10.refs_2_, ...), custom_call_target="tpu_custom_call" | custom-call | tf_op jit(solution)/shard_map/pallas_call | solution.py:553

commit v2 on v1

--- a/solution.py
+++ b/solution.py
@@ -36,39 +36,44 @@
     PHASES.extend([name + "_rs", name + "_ag"])
 
 
-for _name, _m in (("f3", 32), ("f2", 32), ("f1", 16), ("f0", 16), ("g1", 16), ("g2", 32), ("g3", 32)):
+for _name, _m in (("f3", 32), ("f2", 32), ("f1", 16), ("f0", 16), ("g2", 32), ("g3", 32)):
     _rows_ar(_name, _m)
 for _name, _g, _h in (("two", 4, 32), ("one", 8, 16), ("top", 16, 16)):
     if _h == 32:
         _pair(_name + "_rs", _h)
     BUFS["n_" + _name] = (8, 2, _h, N) if _h == 32 else (NR, _h, N)
     BUFS["m_" + _name] = (8, _h, N) if _h == 32 else (NR, _h, N)
-    BUFS["w_" + _name] = (_g, _h, N)
+    BUFS["w_" + _name] = (16 if _g == 8 else _g, _h, N)
     PHASES.extend([_name + "_rs", _name + "_ag"])
 BUFS.update(
     u3=(2, 8, 16, N),
     u2=(2, 8, 16, N),
-    u1=(8, 16, N),
     ru32=(4, 2, 2, 16, N),
     ru31=(8, 2, 16, N),
     ru21=(8, 2, 16, N),
     ru30=(16, 2, 16, N),
     ru20=(16, 2, 16, N),
-    ru10=(16, 16, N),
     bins0=(NR, 16, N),
     bins1=(NR, 16, N),
-    x0p=(16, 16, N),
-    x0l=(16, 16, N),
-    x0r=(NR, 16, N),
-    x0o=(16, 16, N),
-    s10=(2, 16, N),
-    s20=(4, 2, 16, N),
-    s30=(8, 2, 16, N),
-    t10=(16, 16, N),
-    t20=(16, 2, 16, N),
-    t30=(16, 2, 16, N),
-    x1p=(8, 16, N),
-    x1l=(8, 16, N),
+    pg=(8, 256, N),
+    ph=(8, 256, N),
+    wp0=(8, 16, 8, N),
+    wp1=(8, 16, 8, N),
+    ws0=(16, 8, 8, N),
+    ws1=(16, 8, 8, N),
+    nt=(NR, 2, 8, N),
+    mt=(NR, 2, 8, N),
+    wt=(16, 2, 8, N),
+    x0p=(2, 16, 8, N),
+    x0l=(16, 2, 8, N),
+    x0r=(NR, 2, 8, N),
+    x0o=(16, 2, 8, N),
+    s20=(4, 2, 8, N),
+    s30=(8, 2, 8, N),
+    t20=(16, 2, 8, N),
+    t30=(16, 2, 8, N),
+    x1p=(2, 8, 16, N),
+    x1l=(16, 16, N),
     x1r=(NR, 16, N),
     x1o=(16, 16, N),
     s21=(2, 2, 16, N),
@@ -85,7 +90,8 @@
     x3l=(2, 32, N),
     x3o=(16, 32, N),
 )
-PHASES.extend(("u32", "u31", "u21", "u30", "u20", "u10", "x0l", "x0r", "x0o", "t10", "t20", "t30"))
+PHASES.extend(("u32", "u31", "u21", "u30", "u20", "x0l", "x0r", "x0o", "t20", "t30", "tag", "nt", "wt"))
+PHASES.extend(("up1", "up2", "up3", "up4", "dn1", "dn2", "dn3", "pc", "ws0", "ws1"))
 PHASES.extend(("x1l", "x1r", "x1o", "t21", "t31", "x2l", "x2r", "x2o", "t32", "x3l", "x3o", "x2r_c"))
 BUF_NAMES = list(BUFS)
 PHASE_ID = {name: at for at, name in enumerate(PHASES)}
@@ -98,7 +104,7 @@
     ("p2", (512, 256)),
     ("p3", (512, 256)),
 )
-RIGHT = ((256, N), (128, N), (128, N), (64, N))
+RIGHT = ((256, N), (2, 128, N), (128, N), (64, N))
 
 
 def split(value):
@@ -117,7 +123,7 @@
     wlo = dict(zip([name for name, _ in WEIGHTS], refs[at + 7 : at + 14]))
     w32 = dict(zip([name for name, _ in WEIGHTS], refs[at + 14 : at + 21]))
     rhs = refs[at + 21 : at + 25]
-    load_sem, send_sem, recv_sem = refs[at + 25 :]
+    w1hi, w1lo, tag, tag_s, load_sem, tag_sem, send_sem, recv_sem = refs[at + 25 :]
 
     leaf = lax.axis_index("leaf")
     row = lax.axis_index("rows")
@@ -131,9 +137,10 @@
         loads[name].start()
 
     load("i3", weight_in["i3"], w32["i3"])
-    for at, sep in ((3, q3), (2, q2), (1, q1), (0, 0)):
+    for at, sep in ((3, q3), (2, q2), (0, 0)):
         load(at, rhs_in[at].at[sep], rhs[at])
-    for name in ("p3", "i2", "p2", "i1", "p1", "i0"):
+    load(1, rhs_in[1], rhs[1])
+    for name in ("p1", "p3", "i2", "p2", "i1", "i0"):
         load(name, weight_in[name], w32[name])
 
     def ready(*names):
@@ -198,13 +205,48 @@
     def arrived(phase, whole):
         remote(whole, whole, phase, {"rows": lax.rem(row + 1, NR)}).wait_recv()
 
-    def mm(name, x, transposed):
+    def product(high, low, x, transposed):
         xh, xl = split(x)
         both = jnp.concatenate([xh, xl], axis=1)
         dims = (((0,), (0,)), ((), ())) if transposed else (((1,), (0,)), ((), ()))
-        first = lax.dot_general(whi[name][...], both, dims, preferred_element_type=F32)
-        second = lax.dot_general(wlo[name][...], xh, dims, preferred_element_type=F32)
+        first = lax.dot_general(high, both, dims, preferred_element_type=F32)
+        second = lax.dot_general(low, xh, dims, preferred_element_type=F32)
         return first[:, :N] + first[:, N:] + second
+
+    def mm(name, x, transposed):
+        return product(whi[name][...], wlo[name][...], x, transposed)
+
+    pg, ph = buf["pg"], buf["ph"]
+    z_up, z_down = lax.rem(z + 1, 8), lax.rem(z + 7, 8)
+
+    def relay(step):
+        if step > 1:
+            arrived("up%d" % (step - 1), pg.at[0])
+            arrived("dn%d" % (step - 1), pg.at[0])
+        up = w32["p1"] if step == 1 else pg.at[lax.rem(z + 9 - step, 8)]
+        down = w32["p1"] if step == 1 else pg.at[lax.rem(z + step - 1, 8)]
+        mark = "up%d" % step
+        remote(up, pg.at[lax.rem(z + 9 - step, 8)], mark, {"rows": 2 * z_up + core}).start()
+        pending.append((mark, pg.at[0]))
+        if step < 4:
+            mark = "dn%d" % step
+            remote(down, pg.at[lax.rem(z + step - 1, 8)], mark, {"rows": 2 * z_down + core}).start()
+            pending.append((mark, pg.at[0]))
+
+    def relay_end():
+        arrived("up4", pg.at[0])
+        pg[z] = w32["p1"][...]
+        remote(pg, ph, "pc", partner).start()
+        pending.append(("pc", pg))
+
+    def composite(source, out, phase):
+        def one(at, carry):
+            part = product(whi["i1"][...], wlo["i1"][...], source[at], False)
+            out[at] = part.T.reshape(16, 8, N)
+            return carry
+
+        lax.fori_loop(0, 8, one, 0)
+        return leaf_exchange(phase, 16, lambda to: out.at[:, to], buf[phase], out[:, leaf])
 
     def total(ref, count):
         terms = [ref[j] for j in range(count)]
@@ -301,13 +343,30 @@
         loads[1].wait()
         loads[0].wait()
 
-    rows_sum("f3", first, lambda: ready("p3"), ready_two)
+    def send_tags():
+        here = lax.broadcasted_iota(jnp.int32, (8, N), 0)
+        tag[row] = jnp.where(here == 0, r1[0, 0], r1[0, 1])
+        send_tags.some = tag.at[pl.ds(0, NR - 1)]
+        rows_send("tag", lambda peer: tag.at[row], tag.at[row], send_tags.some)
+
+    def slot_one():
+        loads["p1"].wait()
+        relay(1)
+        send_tags()
+        ready("p3")
+
+    def slot_two():
+        relay(2)
+        ready_two()
+
+    rows_sum("f3", first, slot_one, slot_two)
     u3 = buf["u3"]
     u3[...] = mm("p3", rows_value("f3"), True).reshape(u3.shape)
     ru32 = buf["ru32"]
     some = leaf_exchange(
         "u32", 4, lambda to: u3.at[:, pl.ds(2 * to, 2)], ru32, u3[:, pl.ds(2 * pos[4], 2)]
     )
+    relay(3)
     arrived("u32", some)
 
     def bins(dst, terms, base, shape, add=None):
@@ -335,10 +394,13 @@
         start_u3_upper.top = leaf_exchange(
             "u30", 16, lambda to: u3.at[:, lax.rem(to, 8)], ru30, u3[:, pos[8]]
         )
-        ready("i1", "p1", "i0")
+        relay(4)
+        ready("i1", "i0")
 
     piece = pair_reduce("two_rs", buf["n_two"], buf["m_two"], start_u3_upper)
-    leaf_gather("two_ag", 4, piece, buf["w_two"])
+    some = leaf_gather_start("two_ag", 4, piece, buf["w_two"])
+    relay_end()
+    arrived("two_ag", some)
     source = rhs[2][...] - buf["w_two"][...].reshape(128, N)
 
     def fill_one():
@@ -357,11 +419,20 @@
                 terms.append((r3[k, p], ru30[2 * p, k] + ru30[2 * p + 1, k]))
         bins(buf["bins0"], terms, lambda s: 2 * s + q1, (16, N))
 
-    rows_sum("f2", mm("i2", source, True), fill_one, fill_top)
+    def slot_three():
+        slot_three.some = composite(pg, buf["wp0"], "ws0")
+
+    def slot_four():
+        arrived("pc", ph)
+        slot_four.some = composite(ph, buf["wp1"], "ws1")
+
+    rows_sum("f2", mm("i2", source, True), slot_three, slot_four)
     u2 = buf["u2"]
     u2[...] = mm("p2", rows_value("f2"), True).reshape(u2.shape)
     ru21, ru20 = buf["ru21"], buf["ru20"]
     some = leaf_exchange("u21", 8, lambda to: u2.at[:, to], ru21, u2[:, pos[8]])
+    some_top = leaf_exchange("u20", 16, lambda to: u2.at[:, lax.rem(to, 8)], ru20, u2[:, pos[8]])
+    fill_one()
     arrived("u21", some)
     terms = []
     for p in range(2):
@@ -370,81 +441,130 @@
             terms.append((r2[k, 2 * q1 + p], piece))
     bins(buf["n_one"], terms, lambda s: 32 + s, (16, N), buf["bins1"])
 
-    def start_u2_upper():
-        start_u2_upper.top = leaf_exchange(
-            "u20", 16, lambda to: u2.at[:, lax.rem(to, 8)], ru20, u2[:, pos[8]]
-        )
-
-    piece = rows_reduce("one_rs", buf["n_one"], buf["m_one"], start_u2_upper)
-    leaf_gather("one_ag", 8, piece, buf["w_one"])
-    source = rhs[1][...] - buf["w_one"][...].reshape(128, N)
-
     def fill_top_two():
-        arrived("u20", start_u2_upper.top)
+        fill_top()
+        arrived("u20", some_top)
         terms = []
         for p in range(4):
             for k in range(2):
                 piece = (ru20[4 * p, k] + ru20[4 * p + 1, k]) + (ru20[4 * p + 2, k] + ru20[4 * p + 3, k])
                 terms.append((r2[k, p], piece))
-        bins(buf["bins0"], terms, lambda s: 2 * s + q1, (16, N), buf["bins0"])
-
-    rows_sum("f1", mm("i1", source, True), fill_top_two)
-    u1 = buf["u1"]
-    u1[...] = mm("p1", rows_value("f1"), True).reshape(u1.shape)
-    ru10 = buf["ru10"]
-    some = leaf_exchange("u10", 16, lambda to: u1.at[lax.rem(to, 8)], ru10, u1[pos[8]])
-    arrived("u10", some)
+        bins(buf["n_top"], terms, lambda s: 2 * s + q1, (16, N), buf["bins0"])
+        ws0, ws1 = buf["ws0"], buf["ws1"]
+        arrived("ws0", slot_three.some)
+        arrived("ws1", slot_four.some)
+        for p in range(2):
+            halves = []
+            for ws in (ws0, ws1):
+                half = ws[8 * p]
+                for j in range(1, 8):
+                    half = half + ws[8 * p + j]
+                halves.append(half.reshape(64, N))
+            high, low = split(jnp.concatenate(halves, axis=0))
+            w1hi[p] = high
+            w1lo[p] = low
+        arrived("tag", send_tags.some)
+        copy = pltpu.make_async_copy(tag, tag_s, tag_sem)
+        copy.start()
+        copy.wait()
+
+    piece = rows_reduce("one_rs", buf["n_one"], buf["m_one"], fill_top_two)
+    n_top, m_top = buf["n_top"], buf["m_top"]
+    some_one = leaf_gather_start("one_ag", 16, piece, buf["w_one"])
+    some_top = m_top.at[pl.ds(0, NR - 1)]
+    rows_send("top_rs", lambda peer: n_top.at[peer], m_top.at[row], some_top)
+    m_top[row] = n_top[row]
+    arrived("one_ag", some_one)
+    source = [rhs[1][p] - buf["w_one"][pl.ds(8 * p, 8)].reshape(128, N) for p in range(2)]
+
+    def listed(p, k):
+        return tag_s[k, p, 0]
+
+    def block_at(j):
+        return 2 * lax.rem(jnp.int32(j), 8) + (core if j < 8 else 1 - core)
+
+    indices = [[listed(p, block_at(j)) for j in range(16)] for p in range(2)]
     terms = []
     for p in range(2):
-        piece = ru10[8 * p]
-        for j in range(1, 8):
-            piece = piece + ru10[8 * p + j]
-        terms.append((r1[0, p], piece))
-    bins(buf["n_top"], terms, lambda s: 2 * s + q1, (16, N), buf["bins0"])
-    piece = rows_reduce("top_rs", buf["n_top"], buf["m_top"])
-    leaf_gather("top_ag", 16, piece, buf["w_top"])
-    source = rhs[0][...] - buf["w_top"][...].reshape(256, N)
-
-    rows_sum("f0", mm("i0", source, True))
+        update = product(w1hi[p], w1lo[p], source[p], False)
+        terms.extend((indices[p][j], update[8 * j : 8 * j + 8]) for j in range(16))
+    nt = buf["nt"]
+    for s in range(NR):
+        for half in range(2):
+            value = None
+            for index, piece in terms:
+                one = jnp.where(index == 2 * s + half, piece, jnp.zeros((8, N), F32))
+                value = one if value is None else value + one
+            nt[s, half] = value
+
+    f1a, f1b = buf["a_f1"], buf["b_f1"]
+    some_f1 = f1b.at[pl.ds(0, NR - 1)]
+
+    def start_y1():
+        arrived("top_rs", some_top)
+        start_y1.top = leaf_gather_start("top_ag", 16, total(m_top, NR), buf["w_top"])
+        mine = jnp.where(q1 == 0, source[0], source[1])
+        f1a[...] = mm("i1", mine, True).reshape(f1a.shape)
+        rows_send("f1_rs", lambda peer: f1a.at[peer], f1b.at[row], some_f1)
+        f1b[row] = f1a[row]
+
+    piece = rows_reduce("nt", nt, buf["mt"], start_y1)
+    wt = buf["wt"]
+    some = leaf_gather_start("wt", 16, piece, wt)
+    arrived("top_ag", start_y1.top)
+    arrived("wt", some)
+    owed = jnp.concatenate([wt[:, 0].reshape(128, N), wt[:, 1].reshape(128, N)], axis=0)
+    source = rhs[0][...] - (buf["w_top"][...].reshape(256, N) + owed)
+
+    f1y = buf["y_f1"]
+
+    def gather_y1():
+        arrived("f1_rs", some_f1)
+        f1y[row] = total(f1b, NR)
+        gather_y1.some = f1y.at[pl.ds(0, NR - 1)]
+        rows_send("f1_ag", lambda peer: f1y.at[row], f1y.at[row], gather_y1.some)
+
+    def solve_y1():
+        arrived("f1_ag", gather_y1.some)
+        solve_y1.value = mm("i1", rows_value("f1"), False)
+
+    rows_sum("f0", mm("i0", source, True), gather_y1, solve_y1)
     x0p, x0l, x0r = buf["x0p"], buf["x0l"], buf["x0r"]
     x0p[...] = mm("i0", rows_value("f0"), False).reshape(x0p.shape)
-    some = leaf_exchange("x0l", 16, lambda to: x0p.at[to], x0l, x0p[leaf])
+    some = leaf_exchange("x0l", 16, lambda to: x0p.at[:, to], x0l, x0p[:, leaf])
     arrived("x0l", some)
     piece = total(x0l, 16)
     rows_gather("x0r", piece, x0r)
 
     def pick_top(index):
-        held = x0r[jnp.minimum(lax.div(index, 2), 15)]
-        mine = jnp.logical_and(index < 32, lax.rem(index, 2) == q1)
-        return jnp.where(mine, held, jnp.zeros((16, N), F32))
-
-    s10, t10 = buf["s10"], buf["t10"]
+        at = jnp.minimum(index, 31)
+        held = x0r[lax.div(at, 2), lax.rem(at, 2)]
+        return jnp.where(index < 32, held, jnp.zeros((8, N), F32))
+
+    x1p = buf["x1p"]
     for p in range(2):
-        s10[p] = pick_top(r1[0, p])
-    some = leaf_exchange("t10", 16, lambda to: s10.at[lax.div(to, 8)], t10, s10[q1])
+        chosen = jnp.concatenate([pick_top(indices[p][j]) for j in range(16)], axis=0)
+        x1p[p] = -product(w1hi[p], w1lo[p], chosen, True).reshape(8, 16, N)
+    x1p[q1] = x1p[q1] + solve_y1.value.reshape(8, 16, N)
+    x1l, x1r = buf["x1l"], buf["x1r"]
+    some = leaf_exchange("x1l", 16, lambda to: x1p.at[lax.div(to, 8), lax.rem(to, 8)], x1l, x1p[q1, pos[8]])
     wait_x0o = leaf_gather_start("x0o", 16, piece, buf["x0o"])
-    arrived("t10", some)
-    chosen = (t10[pl.ds(0, 8)] + t10[pl.ds(8, 8)]).reshape(128, N)
 
     s20, t20, s30, t30 = buf["s20"], buf["t20"], buf["s30"], buf["t30"]
+    for p in range(4):
+        for k in range(2):
+            s20[p, k] = pick_top(r2[k, p])
+    for p in range(8):
+        for k in range(2):
+            s30[p, k] = pick_top(r3[k, p])
+    arrived("x1l", some)
+    piece = total(x1l, 16)
 
     def fill_t():
-        for p in range(4):
-            for k in range(2):
-                s20[p, k] = pick_top(r2[k, p])
         fill_t.two = leaf_exchange("t20", 16, lambda to: s20.at[lax.div(to, 4)], t20, s20[q2])
-        for p in range(8):
-            for k in range(2):
-                s30[p, k] = pick_top(r3[k, p])
         fill_t.three = leaf_exchange("t30", 16, lambda to: s30.at[lax.div(to, 2)], t30, s30[q3])
 
-    rows_sum("g1", mm("p1", chosen, False), fill_t)
-    x1p, x1l, x1r = buf["x1p"], buf["x1l"], buf["x1r"]
-    x1p[...] = mm("i1", rows_value("f1") - rows_value("g1"), False).reshape(x1p.shape)
-    some = leaf_exchange("x1l", 8, lambda to: x1p.at[to], x1l, x1p[pos[8]])
-    arrived("x1l", some)
-    piece = total(x1l, 8)
-    rows_gather("x1r", piece, x1r)
+    rows_gather("x1r", piece, x1r, fill_t)
 
     def pick_one(index):
         held = x1r[jnp.clip(index - 32, 0, 15)]
@@ -462,7 +582,7 @@
     parts = []
     for k in range(2):
         parts.append(
-            (t20[pl.ds(0, 8), k] + t20[pl.ds(8, 8), k] + t21[pl.ds(0, 8), k]).reshape(128, N)
+            t20[:, k].reshape(128, N) + t21[:, k].reshape(128, N)
         )
 
     def fill_o():
@@ -497,12 +617,13 @@
     arrived("t32", some)
     parts = []
     for k in range(2):
-        upper = t30[pl.ds(0, 8), k] + t30[pl.ds(8, 8), k] + t31[pl.ds(0, 8), k]
-        parts.append(upper.reshape(128, N) + t32[pl.ds(0, 4), k].reshape(128, N))
+        upper = t30[:, k].reshape(128, N) + t31[:, k].reshape(128, N)
+        parts.append(upper + t32[:, k].reshape(128, N))
 
     def outputs():
         arrived("x0o", wait_x0o)
-        out0[...] = buf["x0o"][...].reshape(out0.shape)
+        for half in range(2):
+            out0[0, pl.ds(128 * half, 128)] = buf["x0o"][:, half].reshape(128, N)
         arrived("x1o", wait_x1o)
         out1[...] = buf["x1o"][...].reshape(out1.shape)
         arrived("x2o", wait_x2o)
@@ -542,7 +663,9 @@
             + [pltpu.VMEM(shape, BF16) for _, shape in WEIGHTS] * 2
             + [pltpu.VMEM(shape, F32) for _, shape in WEIGHTS]
             + [pltpu.VMEM(shape, F32) for shape in RIGHT]
-            + [pltpu.SemaphoreType.DMA((11,))]
+            + [pltpu.VMEM((2, 128, 128), BF16)] * 2
+            + [pltpu.VMEM((NR, 8, N), jnp.int32), pltpu.SMEM((NR, 8, N), jnp.int32)]
+            + [pltpu.SemaphoreType.DMA((11,)), pltpu.SemaphoreType.DMA]
             + [pltpu.SemaphoreType.DMA((len(PHASES),)), pltpu.SemaphoreType.DMA((len(PHASES),))],
             compiler_params=pltpu.CompilerParams(
                 collective_id=0, has_side_effects=True, vmem_limit_bytes=60 * 1024 * 1024

time: 200 us -> 180 us (0.900)
  Pallas kernels: 198 us -> 179 us
    pallas_call x1, Pallas kernels: 196 us -> 177 us  [body(): pl.pallas_call(kernel, out_shape=outs, in_specs=[pl.BlockSpec(memory_spac...]
where the time goes in v2:
time: 180 us; the launch traced here: 179 us
  Pallas kernels  179 us (99%)
    pallas_call x1, Pallas kernels, body(): pl.pallas_call(kernel, out_shape=outs, in_specs=[pl.BlockSpec(memory_spac...  177 us

profile of v2, /device:TPU:25, one launch (start us, length us, event | category | flops | bytes accessed | tf_op | source)
XLA Modules:
  0.0 179.5 jit_solution(18000692823246102532)
XLA Ops:
  0.6 176.8 %shard_map.165 = (f32[1,256,128]{2,1,0:T(8,128)}, f32[2,128,128]{2,1,0:T(8,128)}, f32[4,128,128]{2,1,0:T(8,128)}, f32[8,64,128]{2,1,0:T(8,128)}) custom-call(f32[1,256,128]{2,1,0:T(8,128)} %refs_0_.1, f32[2,128,128]{2,1,0:T(8,128)} %refs_1_.1, f32[4,128,128]{2,1,0:T(8,128)} %refs_2_.1, f32[8,64,128]{2,1,0:T(8,128)} %refs_3_.1, f32[256,256]{1,0:T(8,128)} %refs_4_.1, ...), custom_call_target="tpu_custom_call" | custom-call | tf_op jit(solution)/shard_map/pallas_call | solution.py:657
  177.4 2.1 %shard_map.166 = (f32[1,256,128]{2,1,0:T(8,128)}, f32[2,128,128]{2,1,0:T(8,128)}, f32[4,128,128]{2,1,0:T(8,128)}, f32[8,64,128]{2,1,0:T(8,128)}) custom-call(f32[1,256,128]{2,1,0:T(8,128)} %get-tuple-element.8.refs_0_, f32[2,128,128]{2,1,0:T(8,128)} %get-tuple-element.9.refs_1_, f32[4,128,128]{2,1,0:T(8,128)} %get-tuple-element.10.refs_2_, ...), custom_call_target="tpu_custom_call" | custom-call | tf_op jit(solution)/shard_map/pallas_call | solution.py:676

commit v3 on v2

--- a/solution.py
+++ b/solution.py
@@ -36,7 +36,7 @@
     PHASES.extend([name + "_rs", name + "_ag"])
 
 
-for _name, _m in (("f3", 32), ("f2", 32), ("f1", 16), ("f0", 16), ("g2", 32), ("g3", 32)):
+for _name, _m in (("f3", 32), ("f2", 32), ("f1", 16), ("f0", 16), ("g3", 32)):
     _rows_ar(_name, _m)
 for _name, _g, _h in (("two", 4, 32), ("one", 8, 16), ("top", 16, 16)):
     if _h == 32:
@@ -68,31 +68,39 @@
     x0l=(16, 2, 8, N),
     x0r=(NR, 2, 8, N),
     x0o=(16, 2, 8, N),
-    s20=(4, 2, 8, N),
+    qg=(8, N, 512),
+    qh=(8, N, 512),
+    vp0=(8, 2, 8, 16, N),
+    vp1=(8, 2, 8, 16, N),
+    vs0=(8, 4, 2, 16, N),
+    vs1=(8, 4, 2, 16, N),
+    vs2=(8, 4, 2, 16, N),
+    vs3=(8, 4, 2, 16, N),
+    vr=(NR, 2, 2, 16, N),
+    vt=(NR, 2, 2, 16, N),
+    x0e=(2, NR, 2, 8, N),
+    ch2=(2, 32, 16, N),
     s30=(8, 2, 8, N),
-    t20=(16, 2, 8, N),
     t30=(16, 2, 8, N),
     x1p=(2, 8, 16, N),
     x1l=(16, 16, N),
     x1r=(NR, 16, N),
     x1o=(16, 16, N),
-    s21=(2, 2, 16, N),
     s31=(4, 2, 16, N),
-    t21=(8, 2, 16, N),
     t31=(8, 2, 16, N),
-    x2p=(4, 32, N),
-    x2l=(4, 32, N),
+    x2p=(2, 4, 32, N),
+    x2l=(8, 32, N),
     x2r=(8, 2, 32, N),
     x2o=(16, 32, N),
     s32=(2, 2, 32, N),
     t32=(4, 2, 32, N),
-    x3p=(2, 32, N),
-    x3l=(2, 32, N),
-    x3o=(16, 32, N),
+    x3o=(16, 64, N),
 )
-PHASES.extend(("u32", "u31", "u21", "u30", "u20", "x0l", "x0r", "x0o", "t20", "t30", "tag", "nt", "wt"))
+PHASES.extend(("u32", "u31", "u21", "u30", "u20", "x0l", "x0r", "x0o", "t30", "tag", "nt", "wt", "x0e", "vt"))
 PHASES.extend(("up1", "up2", "up3", "up4", "dn1", "dn2", "dn3", "pc", "ws0", "ws1"))
-PHASES.extend(("x1l", "x1r", "x1o", "t21", "t31", "x2l", "x2r", "x2o", "t32", "x3l", "x3o", "x2r_c"))
+PHASES.extend("q%s%d%s" % (way, step, half) for way in ("up", "dn") for step in range(1, 5) for half in "ab")
+PHASES.extend(("qc", "vs0", "vs1", "vs2", "vs3"))
+PHASES.extend(("x1l", "x1r", "x1o", "t31", "x2l", "x2r", "x2o", "t32", "x3o", "x2r_c"))
 BUF_NAMES = list(BUFS)
 PHASE_ID = {name: at for at, name in enumerate(PHASES)}
 WEIGHTS = (
@@ -123,11 +131,15 @@
     wlo = dict(zip([name for name, _ in WEIGHTS], refs[at + 7 : at + 14]))
     w32 = dict(zip([name for name, _ in WEIGHTS], refs[at + 14 : at + 21]))
     rhs = refs[at + 21 : at + 25]
-    w1hi, w1lo, tag, tag_s, load_sem, tag_sem, send_sem, recv_sem = refs[at + 25 :]
+    w1hi, w1lo, w2hi, w2lo, p2hi, p2lo, tag, tag_s, load_sem, tag_sem, send_sem, recv_sem = refs[at + 25 :]
 
     leaf = lax.axis_index("leaf")
     row = lax.axis_index("rows")
     q1, q2, q3 = lax.div(leaf, 8), lax.div(leaf, 4), lax.div(leaf, 2)
+    def eighth(at):
+        return 2 * lax.rem(at, 8) + lax.div(at, 8)
+
+    mine8 = eighth(leaf)
     pos = {16: leaf, 8: lax.rem(leaf, 8), 4: lax.rem(leaf, 4), 2: lax.rem(leaf, 2)}
 
     loads = {}
@@ -219,25 +231,100 @@
     pg, ph = buf["pg"], buf["ph"]
     z_up, z_down = lax.rem(z + 1, 8), lax.rem(z + 7, 8)
 
+    def ring(step, own, land, mark):
+        up, down = mark + "up%d", mark + "dn%d"
+        if step > 1:
+            arrived(up % (step - 1), land.at[0])
+            arrived(down % (step - 1), land.at[0])
+        at = lax.rem(z + 9 - step, 8)
+        src = own if step == 1 else land.at[at]
+        remote(src, land.at[at], up % step, {"rows": 2 * z_up + core}).start()
+        pending.append((up % step, land.at[0]))
+        if step < 4:
+            at = lax.rem(z + step - 1, 8)
+            src = own if step == 1 else land.at[at]
+            remote(src, land.at[at], down % step, {"rows": 2 * z_down + core}).start()
+            pending.append((down % step, land.at[0]))
+
+    def ring_end(own, land, other, mark):
+        arrived(mark + "up4", land.at[0])
+        land[z] = own[...]
+        remote(land, other, mark + "c" if mark else "pc", partner).start()
+        pending.append((mark + "c" if mark else "pc", land))
+
     def relay(step):
+        ring(step, w32["p1"], pg, "")
+
+    qg, qh = buf["qg"], buf["qh"]
+
+    def relay_two(step, half):
+        some, name = pl.ds(64 * half, 64), "ab"[half]
         if step > 1:
-            arrived("up%d" % (step - 1), pg.at[0])
-            arrived("dn%d" % (step - 1), pg.at[0])
-        up = w32["p1"] if step == 1 else pg.at[lax.rem(z + 9 - step, 8)]
-        down = w32["p1"] if step == 1 else pg.at[lax.rem(z + step - 1, 8)]
-        mark = "up%d" % step
-        remote(up, pg.at[lax.rem(z + 9 - step, 8)], mark, {"rows": 2 * z_up + core}).start()
-        pending.append((mark, pg.at[0]))
-        if step < 4:
-            mark = "dn%d" % step
-            remote(down, pg.at[lax.rem(z + step - 1, 8)], mark, {"rows": 2 * z_down + core}).start()
-            pending.append((mark, pg.at[0]))
-
-    def relay_end():
-        arrived("up4", pg.at[0])
-        pg[z] = w32["p1"][...]
-        remote(pg, ph, "pc", partner).start()
-        pending.append(("pc", pg))
+            arrived("qup%d%s" % (step - 1, name), qg.at[0, some])
+            arrived("qdn%d%s" % (step - 1, name), qg.at[0, some])
+        for way, at, to in (("up", z + 9 - step, z_up), ("dn", z + step - 1, z_down)):
+            if step == 4 and (way == "up") != (half == 0):
+                continue
+            mark = "q%s%d%s" % (way, step, name)
+            land = qg.at[lax.rem(at, 8), some]
+            src = w32["i2"].at[some] if step == 1 else land
+            remote(src, land, mark, {"rows": 2 * to + core}).start()
+            pending.append((mark, qg.at[0, some]))
+
+    def relay_two_end():
+        arrived("qup4a", qg.at[0, pl.ds(0, 64)])
+        arrived("qdn4b", qg.at[0, pl.ds(64, 64)])
+        qg[z] = w32["i2"][...]
+        remote(qg, qh, "qc", partner).start()
+        pending.append(("qc", qg))
+
+    def chip_at(step):
+        half = lax.div(step + 1, 2)
+        sign = 2 * lax.rem(step, 2) - 1
+        return lax.rem(z + 8 + half * sign, 8)
+
+    def composite_two(source, out):
+        dims = (((1,), (1,)), ((), ()))
+
+        def one(at, carry):
+            ih, il = split(source[chip_at(at)])
+            first = lax.dot_general(
+                p2hi[...], jnp.concatenate([ih, il], axis=0), dims, preferred_element_type=F32
+            )
+            second = lax.dot_general(p2lo[...], ih, dims, preferred_element_type=F32)
+            out[at] = (first[:, :N] + first[:, N:] + second).reshape(2, 8, 16, N)
+            return carry
+
+        lax.fori_loop(0, 8, one, 0)
+
+    parts_two = []
+
+    def exchange_two(out, half):
+        phase = "vs%d" % len(parts_two)
+        some = pl.ds(4 * half, 4)
+        parts_two.append(
+            leaf_exchange(
+                phase, 8, lambda to: out.at[some, :, to], buf[phase], out[some, :, pos[8]]
+            )
+        )
+
+    vp0, vp1 = buf["vp0"], buf["vp1"]
+
+    vr, vt = buf["vr"], buf["vt"]
+    vt_all = vt.at[pl.ds(0, NR - 1)]
+    pending.append(("vt", vt_all))
+
+    def sum_two(j):
+        arrived("vs%d" % j, parts_two[j])
+        vs = buf["vs%d" % j]
+        side = core if j < 2 else 1 - core
+        for i in range(4):
+            to = 2 * chip_at(jnp.int32(4 * (j % 2) + i)) + side
+            for p in range(2):
+                terms = [vs[4 * p + leaf_at, i] for leaf_at in range(4)]
+                vr[to, p] = (terms[0] + terms[1]) + (terms[2] + terms[3])
+            if j > 0 or i > 0:
+                remote(vr.at[to], vt.at[row], "vt", {"rows": to}).start()
 
     def composite(source, out, phase):
         def one(at, carry):
@@ -246,7 +333,7 @@
             return carry
 
         lax.fori_loop(0, 8, one, 0)
-        return leaf_exchange(phase, 16, lambda to: out.at[:, to], buf[phase], out[:, leaf])
+        return leaf_exchange(phase, 16, lambda to: out.at[:, eighth(to)], buf[phase], out[:, mine8])
 
     def total(ref, count):
         terms = [ref[j] for j in range(count)]
@@ -306,19 +393,21 @@
             fill()
         arrived(phase, some)
 
-    def leaf_gather_start(phase, group, piece, full):
-        full[pos[group]] = piece
+    def leaf_gather_start(phase, group, piece, full, slot=None):
+        slot = pos[group] if slot is None else slot
+        full[slot] = piece
         some = full.at[pl.ds(0, group - 1)]
-        leaf_send(phase, group, lambda to: full.at[pos[group]], full.at[pos[group]], some)
+        leaf_send(phase, group, lambda to: full.at[slot], full.at[slot], some)
         return some
 
     def leaf_gather(phase, group, piece, full):
         arrived(phase, leaf_gather_start(phase, group, piece, full))
 
-    def leaf_exchange(phase, group, src, land, own):
+    def leaf_exchange(phase, group, src, land, own, slot=None):
+        slot = pos[group] if slot is None else slot
         some = land.at[pl.ds(0, group - 1)]
-        leaf_send(phase, group, src, land.at[pos[group]], some)
-        land[pos[group]] = own
+        leaf_send(phase, group, src, land.at[slot], some)
+        land[slot] = own
         return some
 
     def rows_sum(name, value, fill=None, fill2=None):
@@ -344,8 +433,12 @@
         loads[0].wait()
 
     def send_tags():
-        here = lax.broadcasted_iota(jnp.int32, (8, N), 0)
-        tag[row] = jnp.where(here == 0, r1[0, 0], r1[0, 1])
+        here = lax.broadcasted_iota(jnp.int32, (8, N), 1)
+        value = jnp.where(here == 0, r1[0, 0], r1[0, 1])
+        for p in range(4):
+            for k in range(2):
+                value = jnp.where(here == 2 + 2 * p + k, r2[k, p], value)
+        tag[row] = value
         send_tags.some = tag.at[pl.ds(0, NR - 1)]
         rows_send("tag", lambda peer: tag.at[row], tag.at[row], send_tags.some)
 
@@ -399,7 +492,9 @@
 
     piece = pair_reduce("two_rs", buf["n_two"], buf["m_two"], start_u3_upper)
     some = leaf_gather_start("two_ag", 4, piece, buf["w_two"])
-    relay_end()
+    ring_end(w32["p1"], pg, ph, "")
+    relay_two(1, 0)
+    relay_two(1, 1)
     arrived("two_ag", some)
     source = rhs[2][...] - buf["w_two"][...].reshape(128, N)
 
@@ -420,11 +515,14 @@
         bins(buf["bins0"], terms, lambda s: 2 * s + q1, (16, N))
 
     def slot_three():
+        relay_two(2, 0)
         slot_three.some = composite(pg, buf["wp0"], "ws0")
 
     def slot_four():
+        relay_two(2, 1)
         arrived("pc", ph)
         slot_four.some = composite(ph, buf["wp1"], "ws1")
+        fill_top()
 
     rows_sum("f2", mm("i2", source, True), slot_three, slot_four)
     u2 = buf["u2"]
@@ -432,6 +530,9 @@
     ru21, ru20 = buf["ru21"], buf["ru20"]
     some = leaf_exchange("u21", 8, lambda to: u2.at[:, to], ru21, u2[:, pos[8]])
     some_top = leaf_exchange("u20", 16, lambda to: u2.at[:, lax.rem(to, 8)], ru20, u2[:, pos[8]])
+    relay_two(3, 0)
+    relay_two(3, 1)
+    p2hi[...], p2lo[...] = split(w32["p2"][...].T)
     fill_one()
     arrived("u21", some)
     terms = []
@@ -442,7 +543,8 @@
     bins(buf["n_one"], terms, lambda s: 32 + s, (16, N), buf["bins1"])
 
     def fill_top_two():
-        fill_top()
+        relay_two(4, 0)
+        relay_two(4, 1)
         arrived("u20", some_top)
         terms = []
         for p in range(4):
@@ -474,11 +576,13 @@
     some_top = m_top.at[pl.ds(0, NR - 1)]
     rows_send("top_rs", lambda peer: n_top.at[peer], m_top.at[row], some_top)
     m_top[row] = n_top[row]
+    relay_two_end()
+    composite_two(qg, vp0)
     arrived("one_ag", some_one)
     source = [rhs[1][p] - buf["w_one"][pl.ds(8 * p, 8)].reshape(128, N) for p in range(2)]
 
     def listed(p, k):
-        return tag_s[k, p, 0]
+        return tag_s[k, 0, p]
 
     def block_at(j):
         return 2 * lax.rem(jnp.int32(j), 8) + (core if j < 8 else 1 - core)
@@ -501,16 +605,20 @@
     some_f1 = f1b.at[pl.ds(0, NR - 1)]
 
     def start_y1():
+        exchange_two(vp0, 0)
         arrived("top_rs", some_top)
         start_y1.top = leaf_gather_start("top_ag", 16, total(m_top, NR), buf["w_top"])
         mine = jnp.where(q1 == 0, source[0], source[1])
         f1a[...] = mm("i1", mine, True).reshape(f1a.shape)
         rows_send("f1_rs", lambda peer: f1a.at[peer], f1b.at[row], some_f1)
         f1b[row] = f1a[row]
+        arrived("qc", qh)
+        composite_two(qh, vp1)
 
     piece = rows_reduce("nt", nt, buf["mt"], start_y1)
     wt = buf["wt"]
-    some = leaf_gather_start("wt", 16, piece, wt)
+    some = leaf_gather_start("wt", 16, piece, wt, mine8)
+    sum_two(0)
     arrived("top_ag", start_y1.top)
     arrived("wt", some)
     owed = jnp.concatenate([wt[:, 0].reshape(128, N), wt[:, 1].reshape(128, N)], axis=0)
@@ -519,22 +627,26 @@
     f1y = buf["y_f1"]
 
     def gather_y1():
+        exchange_two(vp0, 1)
         arrived("f1_rs", some_f1)
         f1y[row] = total(f1b, NR)
         gather_y1.some = f1y.at[pl.ds(0, NR - 1)]
         rows_send("f1_ag", lambda peer: f1y.at[row], f1y.at[row], gather_y1.some)
 
     def solve_y1():
+        exchange_two(vp1, 0)
         arrived("f1_ag", gather_y1.some)
         solve_y1.value = mm("i1", rows_value("f1"), False)
 
     rows_sum("f0", mm("i0", source, True), gather_y1, solve_y1)
     x0p, x0l, x0r = buf["x0p"], buf["x0l"], buf["x0r"]
     x0p[...] = mm("i0", rows_value("f0"), False).reshape(x0p.shape)
-    some = leaf_exchange("x0l", 16, lambda to: x0p.at[:, to], x0l, x0p[:, leaf])
+    some = leaf_exchange("x0l", 16, lambda to: x0p.at[:, eighth(to)], x0l, x0p[:, mine8])
+    sum_two(1)
+    sum_two(2)
     arrived("x0l", some)
     piece = total(x0l, 16)
-    rows_gather("x0r", piece, x0r)
+    rows_gather("x0r", piece, x0r, lambda: exchange_two(vp1, 1))
 
     def pick_top(index):
         at = jnp.minimum(index, 31)
@@ -548,21 +660,37 @@
     x1p[q1] = x1p[q1] + solve_y1.value.reshape(8, 16, N)
     x1l, x1r = buf["x1l"], buf["x1r"]
     some = leaf_exchange("x1l", 16, lambda to: x1p.at[lax.div(to, 8), lax.rem(to, 8)], x1l, x1p[q1, pos[8]])
-    wait_x0o = leaf_gather_start("x0o", 16, piece, buf["x0o"])
-
-    s20, t20, s30, t30 = buf["s20"], buf["t20"], buf["s30"], buf["t30"]
-    for p in range(4):
-        for k in range(2):
-            s20[p, k] = pick_top(r2[k, p])
+    wait_x0o = leaf_gather_start("x0o", 16, piece, buf["x0o"], mine8)
+    x0e, ch2 = buf["x0e"], buf["ch2"]
+    remote(x0r, x0e.at[q1], "x0e", {"leaf": lax.rem(leaf + 8, 16)}).start()
+    pending.append(("x0e", x0e.at[0]))
+    x0e[q1] = x0r[...]
+
+    sum_two(3)
+    s30, t30 = buf["s30"], buf["t30"]
     for p in range(8):
         for k in range(2):
             s30[p, k] = pick_top(r3[k, p])
     arrived("x1l", some)
     piece = total(x1l, 16)
 
+    indices_two = [
+        [tag_s[k // 2, 0, 2 + 2 * (2 * q1 + p) + k % 2] for k in range(32)] for p in range(2)
+    ]
+
     def fill_t():
-        fill_t.two = leaf_exchange("t20", 16, lambda to: s20.at[lax.div(to, 4)], t20, s20[q2])
-        fill_t.three = leaf_exchange("t30", 16, lambda to: s30.at[lax.div(to, 2)], t30, s30[q3])
+        fill_t.three = leaf_exchange("t30", 16, lambda to: s30.at[lax.div(to, 2)], t30, s30[q3], mine8)
+        fill_t.own = mm("i2", rows_value("f2"), False)
+        arrived("x0e", x0e.at[0])
+        for p in range(2):
+            for k in range(32):
+                at = jnp.minimum(indices_two[p][k], 31)
+                for half in range(2):
+                    ch2[p, k, pl.ds(8 * half, 8)] = x0e[half, lax.div(at, 2), lax.rem(at, 2)]
+        vt[row] = vr[row]
+        arrived("vt", vt_all)
+        for p in range(2):
+            w2hi[p], w2lo[p] = split(vt[:, p].reshape(512, N))
 
     rows_gather("x1r", piece, x1r, fill_t)
 
@@ -571,34 +699,24 @@
         mine = jnp.logical_and(index >= 32, index < 48)
         return jnp.where(mine, held, jnp.zeros((16, N), F32))
 
-    s21, t21, s31, t31 = buf["s21"], buf["t21"], buf["s31"], buf["t31"]
+    x2p, x2l, x2r = buf["x2p"], buf["x2l"], buf["x2r"]
     for p in range(2):
+        for k in range(32):
+            index = indices_two[p][k]
+            ch2[p, k] = jnp.where(index < 32, ch2[p, k], x1r[jnp.clip(index - 32, 0, 15)])
+        x2p[p] = -product(w2hi[p], w2lo[p], ch2[p].reshape(512, N), True).reshape(4, 32, N)
+    x2p[q2 - 2 * q1] = x2p[q2 - 2 * q1] + fill_t.own.reshape(4, 32, N)
+    some = leaf_exchange(
+        "x2l", 8, lambda to: x2p.at[lax.div(to, 4), lax.rem(to, 4)], x2l, x2p[q2 - 2 * q1, pos[4]]
+    )
+    wait_x1o = leaf_gather_start("x1o", 16, piece, buf["x1o"])
+    s31, t31 = buf["s31"], buf["t31"]
+    for p in range(4):
         for k in range(2):
-            s21[p, k] = pick_one(r2[k, 2 * q1 + p])
-    some = leaf_exchange("t21", 8, lambda to: s21.at[lax.div(to, 4)], t21, s21[q2 - 2 * q1])
-    wait_x1o = leaf_gather_start("x1o", 16, piece, buf["x1o"])
-    arrived("t20", fill_t.two)
-    arrived("t21", some)
-    parts = []
-    for k in range(2):
-        parts.append(
-            t20[:, k].reshape(128, N) + t21[:, k].reshape(128, N)
-        )
-
-    def fill_o():
-        for p in range(4):
-            for k in range(2):
-                s31[p, k] = pick_one(r3[k, 4 * q1 + p])
-        fill_o.three = leaf_exchange(
-            "t31", 8, lambda to: s31.at[lax.div(to, 2)], t31, s31[q3 - 4 * q1]
-        )
-
-    rows_sum("g2", mm("p2", jnp.concatenate(parts, axis=0), False), fill_o)
-    x2p, x2l, x2r = buf["x2p"], buf["x2l"], buf["x2r"]
-    x2p[...] = mm("i2", rows_value("f2") - rows_value("g2"), False).reshape(x2p.shape)
-    some = leaf_exchange("x2l", 4, lambda to: x2p.at[to], x2l, x2p[pos[4]])
+            s31[p, k] = pick_one(r3[k, 4 * q1 + p])
+    wait_t31 = leaf_exchange("t31", 8, lambda to: s31.at[lax.div(to, 2)], t31, s31[q3 - 4 * q1])
     arrived("x2l", some)
-    piece = total(x2l, 4)
+    piece = total(x2l, 8)
     pair_gather("x2r", piece, x2r)
 
     def pick_two(index):
@@ -613,7 +731,7 @@
     some = leaf_exchange("t32", 4, lambda to: s32.at[lax.div(to, 2)], t32, s32[q3 - 2 * q2])
     wait_x2o = leaf_gather_start("x2o", 16, piece, buf["x2o"])
     arrived("t30", fill_t.three)
-    arrived("t31", fill_o.three)
+    arrived("t31", wait_t31)
     arrived("t32", some)
     parts = []
     for k in range(2):
@@ -630,12 +748,11 @@
         out2[...] = buf["x2o"][...].reshape(out2.shape)
 
     rows_sum("g3", mm("p3", jnp.concatenate(parts, axis=0), False), outputs)
-    x3p, x3l = buf["x3p"], buf["x3l"]
-    x3p[...] = mm("i3", rows_value("f3") - rows_value("g3"), False).reshape(x3p.shape)
-    some = leaf_exchange("x3l", 2, lambda to: x3p.at[to], x3l, x3p[pos[2]])
-    arrived("x3l", some)
-    leaf_gather("x3o", 16, total(x3l, 2), buf["x3o"])
-    out3[...] = buf["x3o"][...].reshape(out3.shape)
+    x3o = buf["x3o"]
+    part = mm("i3", rows_value("f3") - rows_value("g3"), False)
+    arrived("x3o", leaf_gather_start("x3o", 16, part, x3o))
+    for p in range(8):
+        out3[p] = x3o[2 * p] + x3o[2 * p + 1]
 
     for phase, whole in pending:
         remote(whole, whole, phase, {"rows": lax.rem(row + 1, NR)}).wait_send()
@@ -664,6 +781,8 @@
             + [pltpu.VMEM(shape, F32) for _, shape in WEIGHTS]
             + [pltpu.VMEM(shape, F32) for shape in RIGHT]
             + [pltpu.VMEM((2, 128, 128), BF16)] * 2
+            + [pltpu.VMEM((2, 512, 128), BF16)] * 2
+            + [pltpu.VMEM((256, 512), BF16)] * 2
             + [pltpu.VMEM((NR, 8, N), jnp.int32), pltpu.SMEM((NR, 8, N), jnp.int32)]
             + [pltpu.SemaphoreType.DMA((11,)), pltpu.SemaphoreType.DMA]
             + [pltpu.SemaphoreType.DMA((len(PHASES),)), pltpu.SemaphoreType.DMA((len(PHASES),))],

time: 180 us -> 168 us (0.933)
  Pallas kernels: 179 us -> 167 us
    pallas_call x1, Pallas kernels: 177 us -> 165 us  [body(): pl.pallas_call(kernel, out_shape=outs, in_specs=[pl.BlockSpec(memory_spac...]
where the time goes in v3:
time: 168 us
  Pallas kernels  167 us (99%)
    pallas_call x1, Pallas kernels, body(): pl.pallas_call(kernel, out_shape=outs, in_specs=[pl.BlockSpec(memory_spac...  165 us

profile of v3, /device:TPU:25, one launch (start us, length us, event | category | flops | bytes accessed | tf_op | source)
XLA Modules:
  0.0 168.1 jit_solution(7342213033634711389)
XLA Ops:
  0.6 165.4 %shard_map.165 = (f32[1,256,128]{2,1,0:T(8,128)}, f32[2,128,128]{2,1,0:T(8,128)}, f32[4,128,128]{2,1,0:T(8,128)}, f32[8,64,128]{2,1,0:T(8,128)}) custom-call(f32[1,256,128]{2,1,0:T(8,128)} %refs_0_.1, f32[2,128,128]{2,1,0:T(8,128)} %refs_1_.1, f32[4,128,128]{2,1,0:T(8,128)} %refs_2_.1, f32[8,64,128]{2,1,0:T(8,128)} %refs_3_.1, f32[256,256]{1,0:T(8,128)} %refs_4_.1, ...), custom_call_target="tpu_custom_call" | custom-call | tf_op jit(solution)/shard_map/pallas_call | solution.py:774
  166.0 2.1 %shard_map.166 = (f32[1,256,128]{2,1,0:T(8,128)}, f32[2,128,128]{2,1,0:T(8,128)}, f32[4,128,128]{2,1,0:T(8,128)}, f32[8,64,128]{2,1,0:T(8,128)}) custom-call(f32[1,256,128]{2,1,0:T(8,128)} %get-tuple-element.8.refs_0_, f32[2,128,128]{2,1,0:T(8,128)} %get-tuple-element.9.refs_1_, f32[4,128,128]{2,1,0:T(8,128)} %get-tuple-element.10.refs_2_, ...), custom_call_target="tpu_custom_call" | custom-call | tf_op jit(solution)/shard_map/pallas_call | solution.py:795

commit v4 on v3

--- a/solution.py
+++ b/solution.py
@@ -131,7 +131,7 @@
     wlo = dict(zip([name for name, _ in WEIGHTS], refs[at + 7 : at + 14]))
     w32 = dict(zip([name for name, _ in WEIGHTS], refs[at + 14 : at + 21]))
     rhs = refs[at + 21 : at + 25]
-    w1hi, w1lo, w2hi, w2lo, p2hi, p2lo, tag, tag_s, load_sem, tag_sem, send_sem, recv_sem = refs[at + 25 :]
+    w1hi, w1lo, w2hi, w2lo, p2hi, p2lo, p3hi, p3lo, i2hi, i2lo, i0hi, i0lo, tag, tag_s, load_sem, tag_sem, send_sem, recv_sem = refs[at + 25 :]
 
     leaf = lax.axis_index("leaf")
     row = lax.axis_index("rows")
@@ -427,7 +427,8 @@
     pl.semaphore_wait(barrier, 30)
 
     def ready_two():
-        ready("i2", "p2")
+        loads["i2"].wait()
+        i2hi[...], i2lo[...] = split(w32["i2"][...].T)
         loads[2].wait()
         loads[1].wait()
         loads[0].wait()
@@ -446,7 +447,8 @@
         loads["p1"].wait()
         relay(1)
         send_tags()
-        ready("p3")
+        loads["p3"].wait()
+        p3hi[...], p3lo[...] = split(w32["p3"][...].T)
 
     def slot_two():
         relay(2)
@@ -454,7 +456,7 @@
 
     rows_sum("f3", first, slot_one, slot_two)
     u3 = buf["u3"]
-    u3[...] = mm("p3", rows_value("f3"), True).reshape(u3.shape)
+    u3[...] = product(p3hi[...], p3lo[...], rows_value("f3"), False).reshape(u3.shape)
     ru32 = buf["ru32"]
     some = leaf_exchange(
         "u32", 4, lambda to: u3.at[:, pl.ds(2 * to, 2)], ru32, u3[:, pl.ds(2 * pos[4], 2)]
@@ -488,7 +490,9 @@
             "u30", 16, lambda to: u3.at[:, lax.rem(to, 8)], ru30, u3[:, pos[8]]
         )
         relay(4)
-        ready("i1", "i0")
+        ready("i1")
+        loads["p2"].wait()
+        p2hi[...], p2lo[...] = split(w32["p2"][...].T)
 
     piece = pair_reduce("two_rs", buf["n_two"], buf["m_two"], start_u3_upper)
     some = leaf_gather_start("two_ag", 4, piece, buf["w_two"])
@@ -524,15 +528,16 @@
         slot_four.some = composite(ph, buf["wp1"], "ws1")
         fill_top()
 
-    rows_sum("f2", mm("i2", source, True), slot_three, slot_four)
+    rows_sum("f2", product(i2hi[...], i2lo[...], source, False), slot_three, slot_four)
     u2 = buf["u2"]
-    u2[...] = mm("p2", rows_value("f2"), True).reshape(u2.shape)
+    u2[...] = product(p2hi[...], p2lo[...], rows_value("f2"), False).reshape(u2.shape)
     ru21, ru20 = buf["ru21"], buf["ru20"]
     some = leaf_exchange("u21", 8, lambda to: u2.at[:, to], ru21, u2[:, pos[8]])
     some_top = leaf_exchange("u20", 16, lambda to: u2.at[:, lax.rem(to, 8)], ru20, u2[:, pos[8]])
     relay_two(3, 0)
     relay_two(3, 1)
-    p2hi[...], p2lo[...] = split(w32["p2"][...].T)
+    ready("i0")
+    i0hi[...], i0lo[...] = split(w32["i0"][...].T)
     fill_one()
     arrived("u21", some)
     terms = []
@@ -635,10 +640,12 @@
 
     def solve_y1():
         exchange_two(vp1, 0)
+        whi["i2"][...], wlo["i2"][...] = split(w32["i2"][...])
+        whi["p3"][...], wlo["p3"][...] = split(w32["p3"][...])
         arrived("f1_ag", gather_y1.some)
         solve_y1.value = mm("i1", rows_value("f1"), False)
 
-    rows_sum("f0", mm("i0", source, True), gather_y1, solve_y1)
+    rows_sum("f0", product(i0hi[...], i0lo[...], source, False), gather_y1, solve_y1)
     x0p, x0l, x0r = buf["x0p"], buf["x0l"], buf["x0r"]
     x0p[...] = mm("i0", rows_value("f0"), False).reshape(x0p.shape)
     some = leaf_exchange("x0l", 16, lambda to: x0p.at[:, eighth(to)], x0l, x0p[:, mine8])
@@ -660,7 +667,7 @@
     x1p[q1] = x1p[q1] + solve_y1.value.reshape(8, 16, N)
     x1l, x1r = buf["x1l"], buf["x1r"]
     some = leaf_exchange("x1l", 16, lambda to: x1p.at[lax.div(to, 8), lax.rem(to, 8)], x1l, x1p[q1, pos[8]])
-    wait_x0o = leaf_gather_start("x0o", 16, piece, buf["x0o"], mine8)
+    piece_top = piece
     x0e, ch2 = buf["x0e"], buf["ch2"]
     remote(x0r, x0e.at[q1], "x0e", {"leaf": lax.rem(leaf + 8, 16)}).start()
     pending.append(("x0e", x0e.at[0]))
@@ -679,6 +686,7 @@
     ]
 
     def fill_t():
+        fill_t.out = leaf_gather_start("x0o", 16, piece_top, buf["x0o"], mine8)
         fill_t.three = leaf_exchange("t30", 16, lambda to: s30.at[lax.div(to, 2)], t30, s30[q3], mine8)
         fill_t.own = mm("i2", rows_value("f2"), False)
         arrived("x0e", x0e.at[0])
@@ -709,15 +717,19 @@
     some = leaf_exchange(
         "x2l", 8, lambda to: x2p.at[lax.div(to, 4), lax.rem(to, 4)], x2l, x2p[q2 - 2 * q1, pos[4]]
     )
-    wait_x1o = leaf_gather_start("x1o", 16, piece, buf["x1o"])
+    piece_one = piece
     s31, t31 = buf["s31"], buf["t31"]
     for p in range(4):
         for k in range(2):
             s31[p, k] = pick_one(r3[k, 4 * q1 + p])
-    wait_t31 = leaf_exchange("t31", 8, lambda to: s31.at[lax.div(to, 2)], t31, s31[q3 - 4 * q1])
     arrived("x2l", some)
     piece = total(x2l, 8)
-    pair_gather("x2r", piece, x2r)
+
+    def fill_o():
+        fill_o.three = leaf_exchange("t31", 8, lambda to: s31.at[lax.div(to, 2)], t31, s31[q3 - 4 * q1])
+        fill_o.out = leaf_gather_start("x1o", 16, piece_one, buf["x1o"])
+
+    pair_gather("x2r", piece, x2r, fill_o)
 
     def pick_two(index):
         at = jnp.clip(index - 48, 0, 15)
@@ -729,25 +741,28 @@
         for k in range(2):
             s32[p, k] = pick_two(r3[k, 2 * q2 + p])
     some = leaf_exchange("t32", 4, lambda to: s32.at[lax.div(to, 2)], t32, s32[q3 - 2 * q2])
-    wait_x2o = leaf_gather_start("x2o", 16, piece, buf["x2o"])
+    piece_two = piece
     arrived("t30", fill_t.three)
-    arrived("t31", wait_t31)
+    arrived("t31", fill_o.three)
     arrived("t32", some)
     parts = []
     for k in range(2):
         upper = t30[:, k].reshape(128, N) + t31[:, k].reshape(128, N)
         parts.append(upper + t32[:, k].reshape(128, N))
 
+    def last_out():
+        last_out.some = leaf_gather_start("x2o", 16, piece_two, buf["x2o"])
+
     def outputs():
-        arrived("x0o", wait_x0o)
+        arrived("x0o", fill_t.out)
         for half in range(2):
             out0[0, pl.ds(128 * half, 128)] = buf["x0o"][:, half].reshape(128, N)
-        arrived("x1o", wait_x1o)
+        arrived("x1o", fill_o.out)
         out1[...] = buf["x1o"][...].reshape(out1.shape)
-        arrived("x2o", wait_x2o)
+        arrived("x2o", last_out.some)
         out2[...] = buf["x2o"][...].reshape(out2.shape)
 
-    rows_sum("g3", mm("p3", jnp.concatenate(parts, axis=0), False), outputs)
+    rows_sum("g3", mm("p3", jnp.concatenate(parts, axis=0), False), last_out, outputs)
     x3o = buf["x3o"]
     part = mm("i3", rows_value("f3") - rows_value("g3"), False)
     arrived("x3o", leaf_gather_start("x3o", 16, part, x3o))
@@ -782,7 +797,9 @@
             + [pltpu.VMEM(shape, F32) for shape in RIGHT]
             + [pltpu.VMEM((2, 128, 128), BF16)] * 2
             + [pltpu.VMEM((2, 512, 128), BF16)] * 2
-            + [pltpu.VMEM((256, 512), BF16)] * 2
+            + [pltpu.VMEM((256, 512), BF16)] * 4
+            + [pltpu.VMEM((512, 128), BF16)] * 2
+            + [pltpu.VMEM((256, 256), BF16)] * 2
             + [pltpu.VMEM((NR, 8, N), jnp.int32), pltpu.SMEM((NR, 8, N), jnp.int32)]
             + [pltpu.SemaphoreType.DMA((11,)), pltpu.SemaphoreType.DMA]
             + [pltpu.SemaphoreType.DMA((len(PHASES),)), pltpu.SemaphoreType.DMA((len(PHASES),))],

time: 168 us -> 166 us (0.988)
  Pallas kernels: 167 us -> 165 us
    pallas_call x1, Pallas kernels: 165 us -> 163 us  [body(): pl.pallas_call(kernel, out_shape=outs, in_specs=[pl.BlockSpec(memory_spac...]
where the time goes in v4:
time: 166 us
  Pallas kernels  165 us (99%)
    pallas_call x1, Pallas kernels, body(): pl.pallas_call(kernel, out_shape=outs, in_specs=[pl.BlockSpec(memory_spac...  163 us

profile of v4, /device:TPU:25, one launch (start us, length us, event | category | flops | bytes accessed | tf_op | source)
XLA Modules:
  0.0 165.8 jit_solution(2344698365438862676)
XLA Ops:
  0.6 163.1 %shard_map.165 = (f32[1,256,128]{2,1,0:T(8,128)}, f32[2,128,128]{2,1,0:T(8,128)}, f32[4,128,128]{2,1,0:T(8,128)}, f32[8,64,128]{2,1,0:T(8,128)}) custom-call(f32[1,256,128]{2,1,0:T(8,128)} %refs_0_.1, f32[2,128,128]{2,1,0:T(8,128)} %refs_1_.1, f32[4,128,128]{2,1,0:T(8,128)} %refs_2_.1, f32[8,64,128]{2,1,0:T(8,128)} %refs_3_.1, f32[256,256]{1,0:T(8,128)} %refs_4_.1, ...), custom_call_target="tpu_custom_call" | custom-call | tf_op jit(solution)/shard_map/pallas_call | solution.py:789
  163.8 2.1 %shard_map.166 = (f32[1,256,128]{2,1,0:T(8,128)}, f32[2,128,128]{2,1,0:T(8,128)}, f32[4,128,128]{2,1,0:T(8,128)}, f32[8,64,128]{2,1,0:T(8,128)}) custom-call(f32[1,256,128]{2,1,0:T(8,128)} %get-tuple-element.8.refs_0_, f32[2,128,128]{2,1,0:T(8,128)} %get-tuple-element.9.refs_1_, f32[4,128,128]{2,1,0:T(8,128)} %get-tuple-element.10.refs_2_, ...), custom_call_target="tpu_custom_call" | custom-call | tf_op jit(solution)/shard_map/pallas_call | solution.py:812

commit v5 on v4

--- a/solution.py
+++ b/solution.py
@@ -200,7 +200,7 @@
             remote(src(peer), dst, phase, {"rows": peer}).start()
             return carry
 
-        lax.fori_loop(0, NR - 1, go, 0)
+        lax.fori_loop(0, NR - 1, go, 0, unroll=True)
         pending.append((phase, whole))
 
     def leaf_send(phase, group, src, dst, whole):
@@ -211,7 +211,7 @@
             remote(src(to), dst, phase, {"leaf": base + to}).start()
             return carry
 
-        lax.fori_loop(0, group - 1, go, 0)
+        lax.fori_loop(0, group - 1, go, 0, unroll=True)
         pending.append((phase, whole))
 
     def arrived(phase, whole):
@@ -347,7 +347,7 @@
             remote(src(peer), dst, phase, {"rows": 2 * peer + core}).start()
             return carry
 
-        lax.fori_loop(0, 7, go, 0)
+        lax.fori_loop(0, 7, go, 0, unroll=True)
         pending.append((phase, whole))
 
     def pair_reduce(phase, out, land, fill=None):

time: 166 us -> 166 us (level)
  no operation moved by 1% of the time
where the time goes in v5:
time: 166 us
  Pallas kernels  165 us (99%)
    pallas_call x1, Pallas kernels, body(): pl.pallas_call(kernel, out_shape=outs, in_specs=[pl.BlockSpec(memory_spac...  163 us

profile of v5, /device:TPU:25, one launch (start us, length us, event | category | flops | bytes accessed | tf_op | source)
XLA Modules:
  0.0 166.1 jit_solution(14807939276915149581)
XLA Ops:
  0.6 163.4 %shard_map.165 = (f32[1,256,128]{2,1,0:T(8,128)}, f32[2,128,128]{2,1,0:T(8,128)}, f32[4,128,128]{2,1,0:T(8,128)}, f32[8,64,128]{2,1,0:T(8,128)}) custom-call(f32[1,256,128]{2,1,0:T(8,128)} %refs_0_.1, f32[2,128,128]{2,1,0:T(8,128)} %refs_1_.1, f32[4,128,128]{2,1,0:T(8,128)} %refs_2_.1, f32[8,64,128]{2,1,0:T(8,128)} %refs_3_.1, f32[256,256]{1,0:T(8,128)} %refs_4_.1, ...), custom_call_target="tpu_custom_call" | custom-call | tf_op jit(solution)/shard_map/pallas_call | solution.py:789
  164.0 2.1 %shard_map.166 = (f32[1,256,128]{2,1,0:T(8,128)}, f32[2,128,128]{2,1,0:T(8,128)}, f32[4,128,128]{2,1,0:T(8,128)}, f32[8,64,128]{2,1,0:T(8,128)}) custom-call(f32[1,256,128]{2,1,0:T(8,128)} %get-tuple-element.8.refs_0_, f32[2,128,128]{2,1,0:T(8,128)} %get-tuple-element.9.refs_1_, f32[4,128,128]{2,1,0:T(8,128)} %get-tuple-element.10.refs_2_, ...), custom_call_target="tpu_custom_call" | custom-call | tf_op jit(solution)/shard_map/pallas_call | solution.py:812
